TPU v7x, 32 devices: a whole 2x2x4 slice. The times are simulated.
32 devices in a mesh: pair: 16 (over z, x, core), virt: 2 (over y).
Axes of the slice: x: 2, y: 2, z: 4, core: 2. Of those that a mesh axis runs over, the one named last changes fastest.
Arguments:
- amplitudes: bfloat16 [96, 96, 128, 128], P('pair', None, 'virt'), may hold values from -6 to 6
- integrals: bfloat16 [128, 20, 128, 128], P('virt'), may hold values from -0.125 to 0.125
- cd_tiles: int32 [128, 20], P('virt'), may hold values from 0 to 127, as said below
- tile_counts: int32 [128], P('virt'), may hold values from 10 to 20, as said below
- eps_occ: float32 [96], replicated, may hold values from -2 to -0.5
- eps_virt: float32 [128], replicated, may hold values from 0.5 to 3
Outputs:
- new_amplitudes: bfloat16 [96, 96, 128, 128], P('pair', None, 'virt')
Inputs may be any that keep to these rules, and one draw needn't show every extreme that they name: `cd_tiles`: row a holds 20 different numbers from lo(a) to lo(a) + 2 * 64 - 1, where lo(a) = min(max(a - 64, 0), 0); only its first tile_counts[a] entries are live. `tile_counts`: some entry equals 20.
All inputs are finite; a program needn't handle non-finite values.
Results may differ from a plain program's by a relative error of at most 0.001.
Values may be sent and summed in bfloat16 or wider, within the bound.
A program may use at most 448 MiB of HBM per device.

v0:
```python
import functools

import jax
import jax.numpy as jnp
from jax import lax
from jax.experimental import pallas as pl
from jax.experimental.pallas import tpu as pltpu
from jax.sharding import PartitionSpec as P

MESH = pl.DeviceIdType.MESH
CHUNKS = 6
TOP = 32767.0


def extended(cells, sides, width):
    for axis, dim in sides:
        count = lax.axis_size(axis)
        ends = count - 1
        head = lax.slice_in_dim(cells, 0, width, axis=dim)
        tail = lax.slice_in_dim(cells, cells.shape[dim] - width, cells.shape[dim], axis=dim)
        cells = jnp.concatenate(
            [
                lax.ppermute(tail, axis, [(i, (i + 1) % count) for i in range(ends)]),
                cells,
                lax.ppermute(head, axis, [((i + 1) % count, i) for i in range(ends)]),
            ],
            axis=dim,
        )
    return cells


def general_device(amplitudes, integrals, cd_tiles, tile_counts, eps_occ, eps_virt):
    own_rows = amplitudes.shape[0]
    own_tiles = amplitudes.shape[2]
    slot_count = integrals.shape[1]
    first_tile = lax.axis_index("virt") * own_tiles
    first_row = lax.axis_index("pair") * own_rows
    local_tiles = cd_tiles - first_tile + own_tiles
    slot_ids = lax.broadcasted_iota(jnp.int32, cd_tiles.shape, 1)
    kept_slots = (slot_ids < tile_counts[:, None]).astype(jnp.bfloat16)
    masked_weights = integrals * kept_slots[:, :, None, None]
    padded = extended(amplitudes, (("virt", 2),), own_tiles)
    block_width = min(4, slot_count)
    ladder = None
    for block_start in range(0, slot_count, block_width):
        block_stop = min(block_start + block_width, slot_count)
        columns = local_tiles[:, block_start:block_stop]
        picked = jnp.take(padded, columns, axis=2)
        weights = masked_weights[:, block_start:block_stop]
        term = jnp.einsum("ijasd,asdb->ijab", picked, weights, preferred_element_type=jnp.float32)
        ladder = term if ladder is None else ladder + term
    arrived_ladder = lax.all_to_all(
        lax.all_to_all(ladder, "pair", split_axis=1, concat_axis=0, tiled=True),
        "virt",
        split_axis=3,
        concat_axis=2,
        tiled=True,
    )
    partner = jnp.transpose(arrived_ladder, (1, 0, 3, 2))
    occupied_own = lax.dynamic_slice_in_dim(eps_occ, first_row, own_rows)
    virtual_own = lax.dynamic_slice_in_dim(eps_virt, first_tile, own_tiles)
    denominator = (
        occupied_own[:, None, None, None]
        + eps_occ[None, :, None, None]
        - virtual_own[None, None, :, None]
        - eps_virt[None, None, None, :]
    )
    return ((ladder + partner) / denominator).astype(jnp.bfloat16)


def ladder_kernel(pairs, tiles, own, other, weights, ladder, codes, scales, picked, sems):
    k, h = pl.program_id(0), pl.program_id(1)
    steps, halves = pl.num_programs(0), pl.num_programs(1)
    held = own.shape[0]
    rows, depth = own.shape[1], own.shape[2]
    slots, wide = weights.shape[1], ladder.shape[3]
    half = wide // 2

    @pl.when((k == 0) & (h == 0))
    def _():
        first = pltpu.make_async_copy(own, picked.at[pl.ds(0, held)], sems.at[0])
        second = pltpu.make_async_copy(other, picked.at[pl.ds(held, held)], sems.at[1])
        first.start()
        second.start()
        picked[2 * held] = jnp.zeros((rows, depth), picked.dtype)
        first.wait()
        second.wait()

    for s in range(8):
        a = (h * steps + k) * 8 + s
        lhs = jnp.concatenate([picked[tiles[a, x]] for x in range(slots)], axis=1)
        ladder[h, 0, pl.ds(s, rows, stride=8), :] = jnp.dot(
            lhs, weights[s].reshape(slots * depth, wide), preferred_element_type=jnp.float32
        )

    @pl.when(h == halves - 1)
    def _():
        tall = codes.shape[3]
        low = lax.broadcasted_iota(jnp.int32, (tall, wide), 1) < half

        def largest(p, tops):
            spot = pl.ds(pl.multiple_of(p * tall, 8), tall)
            return tuple(
                jnp.maximum(
                    top,
                    jnp.max(jnp.abs(ladder[x, 0, spot, :]).reshape(tall // 8, 8, wide), axis=0),
                )
                for x, top in enumerate(tops)
            )

        tops = lax.fori_loop(0, pairs, largest, (jnp.zeros((8, wide), jnp.float32),) * 2)
        tops = [jnp.maximum(jnp.max(top, axis=0, keepdims=True), 1e-30) for top in tops]
        sizes = [top / TOP for top in tops]
        factors = [TOP / top for top in tops]
        low_row = low[:1]
        scales[0, pl.ds(k, 1), :] = jnp.where(low_row, sizes[0], pltpu.roll(sizes[1], half, 1))
        scales[1, pl.ds(k, 1), :] = jnp.where(low_row, pltpu.roll(sizes[0], half, 1), sizes[1])

        def pack(p, _):
            spot = pl.ds(pl.multiple_of(p * tall, 8), tall)
            zero, one = (jnp.round(ladder[x, 0, spot, :] * factors[x]) for x in range(2))
            left = jnp.where(low, zero, pltpu.roll(one, half, 1))
            right = jnp.where(low, pltpu.roll(zero, half, 1), one)
            codes[p, 0, 0] = left.astype(jnp.int32).astype(jnp.int16)
            codes[p, 1, 0] = right.astype(jnp.int32).astype(jnp.int16)
            return 0

        lax.fori_loop(0, pairs, pack, 0)


class Exchange:
    def __init__(self, pairs, virts, codes, scales, arrived, sizes, send, recv, send_s, recv_s, own):
        self.refs = codes, scales, arrived, sizes, send, recv, send_s, recv_s
        self.virts, self.count = virts, pairs * virts
        self.here = lax.axis_index("pair"), lax.axis_index("virt")
        p, v = self.here
        self.me = p * virts + v
        self.kept = (
            pltpu.make_async_copy(codes.at[p, v], arrived.at[p, v], own.at[0]),
            pltpu.make_async_copy(scales.at[v], sizes.at[p, v], own.at[1]),
        )

    def target(self, d):
        t = lax.rem(self.me + d, self.count)
        return t // self.virts, lax.rem(t, self.virts)

    def copies(self, d):
        codes, scales, arrived, sizes, send, recv, send_s, recv_s = self.refs
        p, v = self.target(d)
        return (
            pltpu.make_async_remote_copy(
                src_ref=codes.at[p, v],
                dst_ref=arrived.at[self.here],
                send_sem=send.at[d],
                recv_sem=recv.at[d],
                device_id=(p, v),
                device_id_type=MESH,
            ),
            pltpu.make_async_remote_copy(
                src_ref=scales.at[v],
                dst_ref=sizes.at[self.here],
                send_sem=send_s.at[d],
                recv_sem=recv_s.at[d],
                device_id=(p, v),
                device_id_type=MESH,
            ),
        )

    def start(self):
        def begin(d, _):
            for copy in self.copies(d):
                copy.start()
            return 0

        lax.fori_loop(1, self.count, begin, 0)
        for copy in self.kept:
            copy.start()

    def wait(self):
        def finish(d, _):
            for copy in self.copies(d):
                copy.wait()
            return 0

        lax.fori_loop(1, self.count, finish, 0)
        for copy in self.kept:
            copy.wait()


def greet_all(pairs, virts):
    count = pairs * virts
    me = lax.axis_index("pair") * virts + lax.axis_index("virt")
    barrier = pltpu.get_barrier_semaphore()

    def greet(d, _):
        t = lax.rem(me + d, count)
        pl.semaphore_signal(
            barrier, inc=1, device_id=(t // virts, lax.rem(t, virts)), device_id_type=MESH
        )
        return 0

    lax.fori_loop(1, count, greet, 0)
    pl.semaphore_wait(barrier, count - 1)


def exchange_kernel(pairs, virts, *refs):
    moved = Exchange(pairs, virts, *refs)
    greet_all(pairs, virts)
    moved.start()
    moved.wait()


def both_kernel(pairs, virts, beside, more, tiles, own, other, weights, *refs):
    refs = list(refs)
    old = [refs.pop(0) for _ in range(2 * beside)]
    ahead = [refs.pop(0) for _ in range(more)]
    ladder, codes, scales = [refs.pop(0) for _ in range(3)]
    old += [refs.pop(0) for _ in range(2 * beside)]
    ahead += [refs.pop(0) for _ in range(more)]
    picked, sems = refs.pop(0), refs.pop(0)
    tasks = []
    if beside:
        tasks.append(Exchange(pairs, virts, *old, *[refs.pop(0) for _ in range(5)]))
    if more:
        swap_sems = refs.pop(0)
        tasks.append(
            pltpu.make_async_remote_copy(
                src_ref=ahead[0],
                dst_ref=ahead[1],
                send_sem=swap_sems.at[0],
                recv_sem=swap_sems.at[1],
                device_id=(lax.axis_index("pair"), 1 - lax.axis_index("virt")),
                device_id_type=MESH,
            )
        )
    k, h = pl.program_id(0), pl.program_id(1)

    @pl.when((k == 0) & (h == 0))
    def _():
        greet_all(pairs, virts)
        for task in tasks:
            task.start()

    ladder_kernel(pairs, tiles, own, other, weights, ladder, codes, scales, picked, sems)

    @pl.when((k == pl.num_programs(0) - 1) & (h == pl.num_programs(1) - 1))
    def _():
        for task in tasks:
            task.wait()


def combine_kernel(chunks, rows, *refs):
    occ_own, occ_all, virt_own, virt_all = refs[:4]
    ladders = refs[4 : 4 + chunks]
    codes = refs[4 + chunks : 4 + 2 * chunks]
    scales = refs[4 + 2 * chunks : 4 + 3 * chunks]
    out = refs[4 + 3 * chunks]
    values = refs[5 + 3 * chunks]
    p = pl.program_id(0)
    virts, steps, tall, wide = codes[0].shape[1:]
    part = rows // chunks
    quarter = steps * 8
    half = wide // 2
    for r in range(chunks):
        for v in range(virts):
            for k in range(steps):
                values[r, v, k] = codes[r][0, v, k].astype(jnp.float32) * scales[r][0, v, k : k + 1, :]
    low = virt_own[...] + virt_all[...]
    for jj in range(rows):
        chunk, inner = jj // part, jj % part
        for i in range(rows):
            spot = pl.ds((inner * rows + i) * 8, 8)
            tile = values[chunk, :, :, spot, :].reshape(virts * quarter, wide)
            turned = tile.T
            partner = jnp.concatenate(
                [
                    turned[x * half : (x + 1) * half, v * quarter : (v + 1) * quarter]
                    for v in range(virts)
                    for x in range(2)
                ],
                axis=1,
            )
            here = pl.ds(((i % part) * rows + jj) * 8, 8)
            mine = ladders[i // part][:, :, 0, here, :].reshape(2 * quarter, wide)
            level = occ_own[i] + occ_all[p * rows + jj]
            out[i, jj] = ((mine + partner) / (level - low)).astype(out.dtype)


def per_device(amplitudes, integrals, cd_tiles, tile_counts, eps_occ, eps_virt):
    pairs, virts = lax.axis_size("pair"), lax.axis_size("virt")
    rows, others, held, depth = amplitudes.shape
    slots, wide = integrals.shape[1], integrals.shape[3]
    fits = virts == 2 and held % 16 == 0 and rows % CHUNKS == 0
    fits = fits and wide == 2 * held and wide == 128 and (rows // CHUNKS * rows) % 2 == 0
    if not fits:
        return general_device(amplitudes, integrals, cd_tiles, tile_counts, eps_occ, eps_virt)
    part = rows // CHUNKS
    block = part * rows
    count = pairs * block
    tall = block * 8
    steps = held // 16
    first_tile = lax.axis_index("virt") * held
    first_row = lax.axis_index("pair") * rows
    slot_ids = lax.broadcasted_iota(jnp.int32, cd_tiles.shape, 1)
    places = lax.rem(cd_tiles - first_tile + 2 * held, 2 * held)
    tiles = jnp.where(slot_ids < tile_counts[:, None], places, 2 * held)

    ladders, arrived, sizes = [], [], []
    swapped = []
    for r in range(CHUNKS):
        own = amplitudes[r * part : (r + 1) * part].reshape(part, pairs, rows, held, depth)
        own = jnp.transpose(own, (3, 1, 0, 2, 4)).reshape(held, count, depth)
        swapped.append(own)
    other = lax.ppermute(swapped[0], "virt", [(0, 1), (1, 0)])
    anywhere = pl.BlockSpec(memory_space=pl.ANY)
    moved_sems = [pltpu.SemaphoreType.DMA((pairs * virts,))] * 4 + [pltpu.SemaphoreType.DMA((2,))]
    moved_shape = [
        jax.ShapeDtypeStruct((pairs, 2, steps, tall, wide), jnp.int16),
        jax.ShapeDtypeStruct((pairs, 2, 8, wide), jnp.float32),
    ]
    last = ()
    for r in range(CHUNKS):
        own = swapped[r]
        beside = len(last) > 0
        ahead = swapped[r + 1 : r + 2]
        more = len(ahead)
        ladder, *made = pl.pallas_call(
            functools.partial(both_kernel, pairs, virts, beside, more),
            grid_spec=pltpu.PrefetchScalarGridSpec(
                num_scalar_prefetch=1,
                grid=(steps, 2),
                in_specs=[
                    anywhere,
                    anywhere,
                    pl.BlockSpec(
                        (8, slots, depth, wide), lambda k, h, *_: (h * steps + k, 0, 0, 0)
                    ),
                ]
                + [anywhere] * (len(last) + more),
                out_specs=[
                    pl.BlockSpec((2, 1, count * 8, wide), lambda k, h, *_: (0, k, 0, 0)),
                    pl.BlockSpec((pairs, 2, 1, tall, wide), lambda k, h, *_: (0, 0, k, 0, 0)),
                    pl.BlockSpec((2, 8, wide), lambda k, h, *_: (0, 0, 0)),
                ]
                + [anywhere] * (len(last) + more),
                scratch_shapes=[
                    pltpu.VMEM((2 * held + 1, count, depth), amplitudes.dtype),
                    pltpu.SemaphoreType.DMA((2,)),
                ]
                + moved_sems * beside
                + [pltpu.SemaphoreType.DMA((2,))] * more,
            ),
            out_shape=[
                jax.ShapeDtypeStruct((2, steps, count * 8, wide), jnp.float32),
                jax.ShapeDtypeStruct((pairs, 2, steps, tall, wide), jnp.int16),
                jax.ShapeDtypeStruct((2, 8, wide), jnp.float32),
            ]
            + moved_shape * beside
            + [jax.ShapeDtypeStruct(own.shape, own.dtype)] * more,
            cost_estimate=pl.CostEstimate(
                flops=2 * count * held * slots * depth * wide,
                bytes_accessed=2 * integrals.size,
                transcendentals=0,
            ),
            compiler_params=pltpu.CompilerParams(
                vmem_limit_bytes=60 * 2**20, collective_id=r, has_side_effects=True
            ),
            name=f"ladder_{r}",
        )(tiles, own, other, integrals, *last, *ahead)
        last = tuple(made[:2])
        ladders.append(ladder.reshape(2, steps, pairs, tall, wide))
        if beside:
            arrived.append(made[2])
            sizes.append(made[3])
        other = made[-1]
    got, size = pl.pallas_call(
        functools.partial(exchange_kernel, pairs, virts),
        in_specs=[anywhere] * 2,
        out_specs=[anywhere] * 2,
        out_shape=moved_shape,
        scratch_shapes=moved_sems,
        compiler_params=pltpu.CompilerParams(collective_id=CHUNKS, has_side_effects=True),
        name="exchange",
    )(*last)
    arrived.append(got)
    sizes.append(size)
    occ_own = lax.dynamic_slice_in_dim(eps_occ, first_row, rows)
    virt_own = lax.dynamic_slice_in_dim(eps_virt, first_tile, held)
    smem = pl.BlockSpec(memory_space=pltpu.SMEM)
    vmem = pl.BlockSpec(memory_space=pltpu.VMEM)
    return pl.pallas_call(
        functools.partial(combine_kernel, CHUNKS, rows),
        grid=(pairs,),
        in_specs=[smem, smem, vmem, vmem]
        + [pl.BlockSpec((2, steps, 1, tall, wide), lambda p: (0, 0, p, 0, 0))] * CHUNKS
        + [pl.BlockSpec((1, 2, steps, tall, wide), lambda p: (p, 0, 0, 0, 0))] * CHUNKS
        + [pl.BlockSpec((1, 2, 8, wide), lambda p: (p, 0, 0, 0))] * CHUNKS,
        out_specs=pl.BlockSpec((rows, rows, held, wide), lambda p: (0, p, 0, 0)),
        out_shape=jax.ShapeDtypeStruct(amplitudes.shape[:3] + (wide,), jnp.bfloat16),
        scratch_shapes=[pltpu.VMEM((CHUNKS, 2, steps, tall, wide), jnp.float32)],
        name="combine",
    )(
        occ_own,
        eps_occ,
        jnp.broadcast_to(virt_own[:, None], (held, wide)),
        jnp.broadcast_to(eps_virt[None, :], (held, wide)),
        *ladders,
        *arrived,
        *sizes,
    )


def solution(mesh):
    in_specs = (
        P("pair", None, "virt", None),
        P("virt", None, None, None),
        P("virt", None),
        P("virt"),
        P(),
        P(),
    )
    out_specs = P("pair", None, "virt", None)
    return jax.shard_map(
        per_device, mesh=mesh, in_specs=in_specs, out_specs=out_specs, check_vma=False
    )
```

profile of v0, /device:TPU:11, one launch (start us, length us, event | category | flops | bytes accessed | tf_op | source)
XLA Modules:
  0.0 464.2 jit_solution(5057370226176489138)
XLA Ops:
  0.0 6.5 %slice_bitcast_fusion = (bf16[64,96,128]{2,0,1:T(8,128)(2,1)}, bf16[64,96,128]{2,0,1:T(8,128)(2,1)}, bf16[64,96,128]{2,0,1:T(8,128)(2,1)}, bf16[64,96,128]{2,0,1...) fusion(bf16[6,96,64,128]{3,2,1,0:T(8,128)(2,1)} %param.6), kind=kLoop, calls=%fused_computation | loop fusion | bytes 18874368 | tf_op jit(solution)/shard_map/reshape | solution.py:312
  6.5 0.0 copy-start.4
  6.5 1.0 copy.16.own
  7.5 0.0 copy-start
  7.6 1.3 collective-permute-start
  8.9 0.0 copy-done.4
  8.9 0.1 copy.14
  9.0 0.0 copy-start.3
  9.0 3.7 copy.25.refs_2_.own
  12.7 0.0 copy-done
  12.7 0.0 copy-done.3
  12.7 0.0 copy-start.2
  12.7 2.2 copy.21.refs_2_.own
  14.9 0.0 copy-done.2
  14.9 0.0 copy-start.1
  14.9 2.2 copy.19.refs_2_.own
  17.0 0.0 copy-done.1
  17.0 2.2 copy.17.refs_0_.own
  19.2 0.0 copy-start.7
  19.2 0.0 copy-start.6
  19.2 0.0 copy-start.5
  19.2 2.1 copy.23.refs_2_.own
  21.3 0.0 copy-done.7
  21.3 0.7 dynamic_slice.6.refs_0_
  22.0 0.0 copy-done.6
  22.0 0.1 dynamic_slice.7
  22.1 0.0 copy-done.5
  22.1 0.7 fusion.1.tiles
  22.8 20.2 %collective-permute-done.other = bf16[64,96,128]{2,1,0:T(8,128)(2,1)} collective-permute-done((bf16[64,96,128]{2,1,0:T(8,128)(2,1)S(1)}, bf16[64,96,128]{2,1,0:T(8,128)(2,1)}, u32[]{:S(2)}, u32[]{:S(2)}) %collective-permute-start) | collective-permute-done | bytes 1572896 | tf_op jit(solution)/shard_map/ppermute | solution.py:314
  43.0 44.5 %ladder_0.1 = (f32[2,4,768,128]{3,2,1,0:T(8,128)}, s16[16,2,4,48,128]{4,3,2,1,0:T(8,128)(2,1)}, f32[2,8,128]{2,1,0:T(8,128)}, bf16[64,96,128]{2,1,0:T(8,128)(2,1)}) custom-call(s32[64,20]{1,0:T(8,128)} %fusion.1.tiles, bf16[64,96,128]{2,1,0:T(8,128)(2,1)} %copy-done, bf16[64,96,128]{2,1,0:T(8,128)(2,1)} %collective-permute-done.other, ...), custom_call_target="tpu_custom_call" | custom-call | flops 4026531840 | bytes 41943040 | tf_op jit(solution)/shard_map/ladder_0/pallas_call | solution.py:327
  87.6 63.5 %ladder_1.1 = (f32[2,4,768,128]{3,2,1,0:T(8,128)}, s16[16,2,4,48,128]{4,3,2,1,0:T(8,128)(2,1)}, f32[2,8,128]{2,1,0:T(8,128)}, s16[16,2,4,48,128]{4,3,2,1,0:T(8,1...) custom-call(s32[64,20]{1,0:T(8,128)} %fusion.1.tiles, bf16[64,96,128]{2,1,0:T(8,128)(2,1)} %copy.17.refs_0_.own, ...), custom_call_target="tpu_custom_call" | custom-call | flops 4026531840 | bytes 41943040 | tf_op jit(solution)/shard_map/ladder_1/pallas_call | solution.py:327
  151.0 64.0 %ladder_2.1 = (f32[2,4,768,128]{3,2,1,0:T(8,128)}, s16[16,2,4,48,128]{4,3,2,1,0:T(8,128)(2,1)}, f32[2,8,128]{2,1,0:T(8,128)}, s16[16,2,4,48,128]{4,3,2,1,0:T(8,1...) custom-call(s32[64,20]{1,0:T(8,128)} %fusion.1.tiles, bf16[64,96,128]{2,1,0:T(8,128)(2,1)} %copy.19.refs_2_.own, ...), custom_call_target="tpu_custom_call" | custom-call | flops 4026531840 | bytes 41943040 | tf_op jit(solution)/shard_map/ladder_2/pallas_call | solution.py:327
  215.0 63.0 %ladder_3.1 = (f32[2,4,768,128]{3,2,1,0:T(8,128)}, s16[16,2,4,48,128]{4,3,2,1,0:T(8,128)(2,1)}, f32[2,8,128]{2,1,0:T(8,128)}, s16[16,2,4,48,128]{4,3,2,1,0:T(8,1...) custom-call(s32[64,20]{1,0:T(8,128)} %fusion.1.tiles, bf16[64,96,128]{2,1,0:T(8,128)(2,1)} %copy.21.refs_2_.own, ...), custom_call_target="tpu_custom_call" | custom-call | flops 4026531840 | bytes 41943040 | tf_op jit(solution)/shard_map/ladder_3/pallas_call | solution.py:327
  278.1 63.6 %ladder_4.1 = (f32[2,4,768,128]{3,2,1,0:T(8,128)}, s16[16,2,4,48,128]{4,3,2,1,0:T(8,128)(2,1)}, f32[2,8,128]{2,1,0:T(8,128)}, s16[16,2,4,48,128]{4,3,2,1,0:T(8,1...) custom-call(s32[64,20]{1,0:T(8,128)} %fusion.1.tiles, bf16[64,96,128]{2,1,0:T(8,128)(2,1)} %copy.23.refs_2_.own, ...), custom_call_target="tpu_custom_call" | custom-call | flops 4026531840 | bytes 41943040 | tf_op jit(solution)/shard_map/ladder_4/pallas_call | solution.py:327
  341.7 48.5 %ladder_5.1 = (f32[2,4,768,128]{3,2,1,0:T(8,128)}, s16[16,2,4,48,128]{4,3,2,1,0:T(8,128)(2,1)}, f32[2,8,128]{2,1,0:T(8,128)}, s16[16,2,4,48,128]{4,3,2,1,0:T(8,128)(2,1)}, f32[16,2,8,128]{3,2,1,0:T(8,128)}) custom-call(s32[64,20]{1,0:T(8,128)} %fusion.1.tiles, bf16[64,96,128]{2,1,0:T(8,128)(2,1)} %copy.25.refs_2_.own, ...), custom_call_target="tpu_custom_call" | custom-call | flops 4026531840 | bytes 41943040 | tf_op jit(solution)/shard_map/ladder_5/pallas_call | solution.py:327
  390.2 42.4 %exchange.1 = (s16[16,2,4,48,128]{4,3,2,1,0:T(8,128)(2,1)}, f32[16,2,8,128]{3,2,1,0:T(8,128)}) custom-call(s16[16,2,4,48,128]{4,3,2,1,0:T(8,128)(2,1)} %get-tuple-element.66.refs_0_, f32[2,8,128]{2,1,0:T(8,128)} %get-tuple-element.67.refs_1_), custom_call_target="tpu_custom_call" | custom-call | tf_op jit(solution)/shard_map/exchange/pallas_call | solution.py:376
  432.7 0.7 broadcast_in_dim.6.refs_2_
  433.4 0.6 broadcast_in_dim.7.refs_3_
  434.0 30.1 %combine.1 = bf16[6,96,64,128]{3,2,1,0:T(8,128)(2,1)} custom-call(f32[6]{0:T(128)} %dynamic_slice.6.refs_0_, f32[96]{0:T(128)} %refs_1_.1, f32[64,128]{1,0:T(8,128)} %broadcast_in_dim.6.refs_2_, f32[64,128]{1,0:T(8,128)} %broadcast_in_dim.7.refs_3_, f32[2,4,16,48,128]{4,3,2,1,0:T(8,128)} %bitcast.42, f32[2,4,16,48,128]{4,3,2,1,0:T(8,128)} %bitcast.43, ...), custom_call_target="tpu_custom_call" | custom-call | tf_op jit(solution)/shard_map/combine/pallas_call | solution.py:391
Async XLA Ops:
  6.5 2.3 copy-start.4
  7.5 5.1 %copy-start = (bf16[64,96,128]{2,1,0:T(8,128)(2,1)}, bf16[64,96,128]{2,1,0:T(8,128)(2,1)S(1)}, u32[]{:S(2)}) copy-start(bf16[64,96,128]{2,1,0:T(8,128)(2,1)S(1)} %copy.16.own) | copy-start | bytes 4718596
  7.6 35.5 %collective-permute-start = (bf16[64,96,128]{2,1,0:T(8,128)(2,1)S(1)}, bf16[64,96,128]{2,1,0:T(8,128)(2,1)}, u32[]{:S(2)}, u32[]{:S(2)}) collective-permute-start(bf16[64,96,128]{2,1,0:T(8,128)(2,1)S(1)} %copy.16.own), channel_id=1, source_target_pairs={{0,1},{1,0},{2,3},{3,2},{4,5},{5,4},{6,7},{7,6},{8,9},{9,8},{10,11... | collective-permute-start | bytes 4718600 | tf_op jit(solution)/shard_map/ppermute | solution.py:314
  9.0 3.7 copy-start.3
  12.7 2.2 copy-start.2
  14.9 2.2 copy-start.1
  19.2 2.2 copy-start.7
  19.2 2.8 copy-start.6
  19.2 2.9 copy-start.5
where the time goes:
time: 466 us; the launch traced here: 464 us
  Pallas kernels  420 us (90%)
  local copies, waits for them, and re-layouts  22 us (5%)
  waiting for transfers between devices  20.2 us (4%)
    pallas_call x6, Pallas kernels, per_device(): pl.pallas_call(functools.partial(both_kernel, pairs, virts, beside, more)...  347 us
    pallas_call x1, Pallas kernels, per_device(): pl.pallas_call(functools.partial(exchange_kernel, pairs, virts), in_specs...  42.4 us
    pallas_call x1, Pallas kernels, per_device(): pl.pallas_call(functools.partial(combine_kernel, CHUNKS, rows), grid=(pai...  30.1 us
    ppermute x1, waiting for transfers between devices, per_device(): other = lax.ppermute(swapped[0], 'virt', [(0, 1), (1, 0)])  20.2 us
    reshape x7, local copies, waits for them, and re-layouts, per_device(): own = jnp.transpose(own, (3, 1, 0, 2, 4)).reshape(held, count, depth)  19.9 us
  transfers between devices with their start and end apart: 1, of which 1 were waited for; matrix products, arithmetic and copies ran while one was open for 3% of the time, Pallas kernels for 0%

commit v1 on v0

v1 whole, which is shorter than its diff:
```python
import functools

import jax
import jax.numpy as jnp
from jax import lax
from jax.experimental import pallas as pl
from jax.experimental.pallas import tpu as pltpu
from jax.sharding import PartitionSpec as P

MESH = pl.DeviceIdType.MESH
STEP = 8
TOP = 32767.0


def extended(cells, sides, width):
    for axis, dim in sides:
        count = lax.axis_size(axis)
        ends = count - 1
        head = lax.slice_in_dim(cells, 0, width, axis=dim)
        tail = lax.slice_in_dim(cells, cells.shape[dim] - width, cells.shape[dim], axis=dim)
        cells = jnp.concatenate(
            [
                lax.ppermute(tail, axis, [(i, (i + 1) % count) for i in range(ends)]),
                cells,
                lax.ppermute(head, axis, [((i + 1) % count, i) for i in range(ends)]),
            ],
            axis=dim,
        )
    return cells


def general_device(amplitudes, integrals, cd_tiles, tile_counts, eps_occ, eps_virt):
    own_rows = amplitudes.shape[0]
    own_tiles = amplitudes.shape[2]
    slot_count = integrals.shape[1]
    first_tile = lax.axis_index("virt") * own_tiles
    first_row = lax.axis_index("pair") * own_rows
    local_tiles = cd_tiles - first_tile + own_tiles
    slot_ids = lax.broadcasted_iota(jnp.int32, cd_tiles.shape, 1)
    kept_slots = (slot_ids < tile_counts[:, None]).astype(jnp.bfloat16)
    masked_weights = integrals * kept_slots[:, :, None, None]
    padded = extended(amplitudes, (("virt", 2),), own_tiles)
    block_width = min(4, slot_count)
    ladder = None
    for block_start in range(0, slot_count, block_width):
        block_stop = min(block_start + block_width, slot_count)
        columns = local_tiles[:, block_start:block_stop]
        picked = jnp.take(padded, columns, axis=2)
        weights = masked_weights[:, block_start:block_stop]
        term = jnp.einsum("ijasd,asdb->ijab", picked, weights, preferred_element_type=jnp.float32)
        ladder = term if ladder is None else ladder + term
    arrived_ladder = lax.all_to_all(
        lax.all_to_all(ladder, "pair", split_axis=1, concat_axis=0, tiled=True),
        "virt",
        split_axis=3,
        concat_axis=2,
        tiled=True,
    )
    partner = jnp.transpose(arrived_ladder, (1, 0, 3, 2))
    occupied_own = lax.dynamic_slice_in_dim(eps_occ, first_row, own_rows)
    virtual_own = lax.dynamic_slice_in_dim(eps_virt, first_tile, own_tiles)
    denominator = (
        occupied_own[:, None, None, None]
        + eps_occ[None, :, None, None]
        - virtual_own[None, None, :, None]
        - eps_virt[None, None, None, :]
    )
    return ((ladder + partner) / denominator).astype(jnp.bfloat16)


def greet_all(pairs, virts):
    count = pairs * virts
    me = lax.axis_index("pair") * virts + lax.axis_index("virt")
    barrier = pltpu.get_barrier_semaphore()

    def greet(d, _):
        t = lax.rem(me + d, count)
        pl.semaphore_signal(
            barrier, inc=1, device_id=(t // virts, lax.rem(t, virts)), device_id_type=MESH
        )
        return 0

    lax.fori_loop(1, count, greet, 0)
    pl.semaphore_wait(barrier, count - 1)


def turn_tiles(block, picked, first):
    tall, held = block.shape[0], block.shape[1]

    def turn(x, _):
        rows = pl.ds(pl.multiple_of(x * 16, 16), 16)
        for c in range(0, held, 16):
            picked[pl.ds(first + c, 16), rows, :] = jnp.swapaxes(block[rows, pl.ds(c, 16), :], 0, 1)
        return 0

    lax.fori_loop(0, tall // 16, turn, 0)


def pack(pairs, mine, codes, scales):
    held, wide = codes.shape[2], codes.shape[3]
    duos = codes.shape[1]
    half = wide // 2
    low = lax.broadcasted_iota(jnp.int32, (held, wide), 1) < half
    low_row = low[:1]

    def one(p, _):
        for m in range(duos):
            tiles, sizes = [], []
            for e in range(2):
                spot = pl.ds(pl.multiple_of((p * 2 * duos + 2 * m + e) * held, 8), held)
                tile = mine[spot, :]
                top = jnp.maximum(jnp.max(jnp.abs(tile), axis=0, keepdims=True), 1e-30)
                tiles.append(jnp.round(tile * (TOP / top)))
                sizes.append(top / TOP)
            for v in range(2):
                moved = [
                    x if v == e else pltpu.roll(x, half, 1) for e, x in enumerate(tiles)
                ]
                code = jnp.where(low, moved[0], moved[1])
                codes[2 * p + v, m] = code.astype(jnp.int32).astype(jnp.int16)
                turned = [
                    x if v == e else pltpu.roll(x, half, 1) for e, x in enumerate(sizes)
                ]
                scales[2 * p + v, pl.ds(m, 1), :] = jnp.where(low_row, turned[0], turned[1])
        return 0

    lax.fori_loop(0, pairs, one, 0)


def fused_kernel(pairs, virts, *refs):
    tiles, occ_own, occ_all, amplitudes, weights, virt_own, virt_all = refs[:7]
    out, codes_far, scales_far = refs[7:10]
    own, other, picked, ladder, codes, scales, arrived, sizes, results = refs[10:19]
    own_sem, swap_send, swap_recv, hop, send, recv, send_s, recv_s, out_sem = refs[19:]
    r, k = pl.program_id(0), pl.program_id(1)
    rows, steps = pl.num_programs(0), pl.num_programs(1)
    chunks, others, held, depth = amplitudes.shape
    block, slots, _, wide = weights.shape
    count = pairs * virts
    p, v = lax.axis_index("pair"), lax.axis_index("virt")
    me = p * virts + v
    duos = codes.shape[1]

    def own_copy(x):
        return pltpu.make_async_copy(amplitudes.at[x], own, own_sem)

    def swap(x):
        return pltpu.make_async_remote_copy(
            src_ref=amplitudes.at[x],
            dst_ref=other.at[x],
            send_sem=swap_send.at[x],
            recv_sem=swap_recv.at[x],
            device_id=(p, 1 - v),
            device_id_type=MESH,
        )

    def moves(x, d):
        t = lax.rem(me + d, count)
        target = (t // virts, lax.rem(t, virts))
        return [
            pltpu.make_async_remote_copy(
                src_ref=source.at[x, t],
                dst_ref=land.at[x, me],
                send_sem=sent.at[x],
                recv_sem=got.at[x],
                device_id=target,
                device_id_type=MESH,
            )
            for source, land, sent, got in (
                (codes_far, arrived, send, recv),
                (scales_far, sizes, send_s, recv_s),
            )
        ]

    @pl.when((r == 0) & (k == 0))
    def _():
        own_copy(0).start()
        greet_all(pairs, virts)
        for x in range(chunks):
            swap(x).start()
        picked[2 * held] = jnp.zeros((others, depth), picked.dtype)

    @pl.when(k == 0)
    def _():
        own_copy(r).wait()
        turn_tiles(own, picked, 0)
        swap(r).wait_recv()
        turn_tiles(other.at[r], picked, held)

        @pl.when(r + 1 < rows)
        def _():
            own_copy(r + 1).start()

    for s in range(block):
        a = k * block + s
        lhs = jnp.concatenate([picked[tiles[a, x]] for x in range(slots)], axis=1)
        ladder[r, pl.ds(a, others, stride=held), :] = jnp.dot(
            lhs, weights[s].reshape(slots * depth, wide), preferred_element_type=jnp.float32
        )

    @pl.when(k == steps - 1)
    def _():
        pack(pairs, ladder.at[r], codes, scales)
        hops = (
            pltpu.make_async_copy(codes, codes_far.at[r], hop.at[0]),
            pltpu.make_async_copy(scales, scales_far.at[r], hop.at[1]),
        )
        for copy in hops:
            copy.start()
        for copy in hops:
            copy.wait()

        def begin(d, _):
            for copy in moves(r, d):
                copy.start()
            return 0

        lax.fori_loop(1, count, begin, 0)
        pltpu.make_async_copy(codes_far.at[r, me], arrived.at[r, me], recv.at[r]).start()
        pltpu.make_async_copy(scales_far.at[r, me], sizes.at[r, me], recv_s.at[r]).start()

    @pl.when((r == rows - 1) & (k == steps - 1))
    def _():
        low = virt_own[...] + virt_all[...]

        def result(n):
            slot = lax.rem(n, 2)
            j = lax.rem(n, pairs) * chunks + n // pairs
            return pltpu.make_async_copy(results.at[slot], out.at[:, j], out_sem.at[slot])

        def combine(n, _):
            c, q = n // pairs, lax.rem(n, pairs)
            slot = lax.rem(n, 2)

            @pl.when(q == 0)
            def _():
                pltpu.make_async_copy(arrived.at[c], arrived.at[c], recv.at[c]).wait()
                pltpu.make_async_copy(sizes.at[c], sizes.at[c], recv_s.at[c]).wait()

            @pl.when(n >= 2)
            def _():
                result(n - 2).wait()

            j = q * chunks + c
            for m in range(duos):
                tile = jnp.concatenate(
                    [
                        arrived[c, 2 * q + x, m].astype(jnp.float32)
                        * sizes[c, 2 * q + x, pl.ds(m, 1), :]
                        for x in range(virts)
                    ],
                    axis=0,
                )
                turned = tile.T
                for e in range(2):
                    i = 2 * m + e
                    mine = ladder[i, pl.ds(pl.multiple_of(j * held, 8), held), :]
                    level = occ_own[i] + occ_all[j]
                    partner = turned[e * held : (e + 1) * held]
                    results[slot, i] = ((mine + partner) / (level - low)).astype(results.dtype)
            result(n).start()
            return 0

        total = chunks * pairs
        lax.fori_loop(0, total, combine, 0)
        result(total - 2).wait()
        result(total - 1).wait()
        for x in range(chunks):
            swap(x).wait_send()
            most = pl.ds(0, count - 1)
            pltpu.make_async_copy(codes_far.at[x, most], codes_far.at[x, most], send.at[x]).wait()
            pltpu.make_async_copy(scales_far.at[x, most], scales_far.at[x, most], send_s.at[x]).wait()


def per_device(amplitudes, integrals, cd_tiles, tile_counts, eps_occ, eps_virt):
    pairs, virts = lax.axis_size("pair"), lax.axis_size("virt")
    rows, others, held, depth = amplitudes.shape
    slots, wide = integrals.shape[1], integrals.shape[3]
    fits = virts == 2 and held % 16 == 0 and rows % 2 == 0 and rows <= 16 and others % 16 == 0
    fits = fits and wide == 2 * held and wide == 128 and held % STEP == 0
    if not fits:
        return general_device(amplitudes, integrals, cd_tiles, tile_counts, eps_occ, eps_virt)
    count = pairs * virts
    duos = rows // 2
    steps = held // STEP
    first_tile = lax.axis_index("virt") * held
    first_row = lax.axis_index("pair") * rows
    slot_ids = lax.broadcasted_iota(jnp.int32, cd_tiles.shape, 1)
    places = lax.rem(cd_tiles - first_tile + 2 * held, 2 * held)
    tiles = jnp.where(slot_ids < tile_counts[:, None], places, 2 * held)
    occ_own = lax.dynamic_slice_in_dim(eps_occ, first_row, rows)
    virt_own = lax.dynamic_slice_in_dim(eps_virt, first_tile, held)
    anywhere = pl.BlockSpec(memory_space=pl.ANY)
    vmem = pl.BlockSpec(memory_space=pltpu.VMEM)
    code_shape = (count, duos, held, wide)
    scale_shape = (count, 8, wide)
    flops = 2 * rows * others * held * slots * depth * wide
    out, _, _ = pl.pallas_call(
        functools.partial(fused_kernel, pairs, virts),
        grid_spec=pltpu.PrefetchScalarGridSpec(
            num_scalar_prefetch=3,
            grid=(rows, steps),
            in_specs=[
                anywhere,
                pl.BlockSpec((STEP, slots, depth, wide), lambda r, k, *_: (k, 0, 0, 0)),
                vmem,
                vmem,
            ],
            out_specs=[anywhere] * 3,
            scratch_shapes=[
                pltpu.VMEM((others, held, depth), amplitudes.dtype),
                pltpu.VMEM((rows, others, held, depth), amplitudes.dtype),
                pltpu.VMEM((2 * held + 1, others, depth), amplitudes.dtype),
                pltpu.VMEM((rows, others * held, wide), jnp.float32),
                pltpu.VMEM(code_shape, jnp.int16),
                pltpu.VMEM(scale_shape, jnp.float32),
                pltpu.VMEM((rows,) + code_shape, jnp.int16),
                pltpu.VMEM((rows,) + scale_shape, jnp.float32),
                pltpu.VMEM((2, rows, held, wide), jnp.bfloat16),
                pltpu.SemaphoreType.DMA,
                pltpu.SemaphoreType.DMA((rows,)),
                pltpu.SemaphoreType.DMA((rows,)),
                pltpu.SemaphoreType.DMA((2,)),
                pltpu.SemaphoreType.DMA((rows,)),
                pltpu.SemaphoreType.DMA((rows,)),
                pltpu.SemaphoreType.DMA((rows,)),
                pltpu.SemaphoreType.DMA((rows,)),
                pltpu.SemaphoreType.DMA((2,)),
            ],
        ),
        out_shape=[
            jax.ShapeDtypeStruct(amplitudes.shape[:3] + (wide,), jnp.bfloat16),
            jax.ShapeDtypeStruct((rows,) + code_shape, jnp.int16),
            jax.ShapeDtypeStruct((rows,) + scale_shape, jnp.float32),
        ],
        cost_estimate=pl.CostEstimate(
            flops=flops, bytes_accessed=2 * rows * integrals.size, transcendentals=0
        ),
        compiler_params=pltpu.CompilerParams(
            vmem_limit_bytes=63 * 2**20, collective_id=0, has_side_effects=True
        ),
        name="ladder",
    )(
        tiles,
        occ_own,
        eps_occ,
        amplitudes,
        integrals,
        jnp.broadcast_to(virt_own[:, None], (held, wide)),
        jnp.broadcast_to(eps_virt[None, :], (held, wide)),
    )
    return out


def solution(mesh):
    in_specs = (
        P("pair", None, "virt", None),
        P("virt", None, None, None),
        P("virt", None),
        P("virt"),
        P(),
        P(),
    )
    out_specs = P("pair", None, "virt", None)
    return jax.shard_map(
        per_device, mesh=mesh, in_specs=in_specs, out_specs=out_specs, check_vma=False
    )
```

time: 466 us -> 375 us (0.80)
  Pallas kernels: 420 us -> 353 us
  waiting for transfers between devices: 20.2 us -> 0 us
  local copies, waits for them, and re-layouts: 22 us -> 16 us
    pallas_call x8 -> x1, Pallas kernels: 420 us -> 353 us  [per_device(): pl.pallas_call(functools.partial(fused_kernel, pairs, virts), grid_spec=p...]
    ppermute x1 -> x0, waiting for transfers between devices: 20.2 us -> none  [per_device(): other = lax.ppermute(swapped[0], 'virt', [(0, 1), (1, 0)])]
    reshape x7 -> x0, local copies, waits for them, and re-layouts: 19.9 us -> none  [per_device(): own = jnp.transpose(own, (3, 1, 0, 2, 4)).reshape(held, count, depth)]
    unnamed x17 -> x2, local copies, waits for them, and re-layouts: 0.12 us -> 12.1 us
  transfers between devices with their start and end apart: 1 -> 0, of which waited for: 1 -> 0; matrix products, arithmetic and copies ran while one was open for 3% -> 0% of each run, Pallas kernels for 0% -> 0%
where the time goes in v1:
time: 375 us; the launch traced here: 371 us
  Pallas kernels  353 us (94%)
  local copies, waits for them, and re-layouts  16 us (4%)
    pallas_call x1, Pallas kernels, per_device(): pl.pallas_call(functools.partial(fused_kernel, pairs, virts), grid_spec=p...  353 us
    unnamed x2, local copies, waits for them, and re-layouts  12.1 us

profile of v1, /device:TPU:11, one launch (start us, length us, event | category | flops | bytes accessed | tf_op | source)
XLA Modules:
  0.0 370.8 jit_solution(15787700167497062563)
XLA Ops:
  0.0 1.2 dynamic_slice.6.refs_1_
  1.2 0.7 dynamic_slice.7
  2.0 0.7 broadcast_in_dim.6.refs_5_
  2.6 0.8 copy.7
  3.4 1.3 fusion.1.refs_0_
  4.8 1.3 broadcast_in_dim.7.refs_6_
  6.0 353.4 %ladder.1 = (bf16[6,96,64,128]{3,2,1,0:T(8,128)(2,1)}, s16[6,32,3,64,128]{4,3,2,1,0:T(8,128)(2,1)}, f32[6,32,8,128]{3,2,1,0:T(8,128)}) custom-call(s32[64,20]{1,0:T(8,128)} %fusion.1.refs_0_, f32[6]{0:T(128)} %dynamic_slice.6.refs_1_, f32[96]{0:T(128)} %refs_2_.1, bf16[6,96,64,128]{3,2,1,0:T(8,128)(2,1)} %refs_3_.1, bf16[64,20,128,128]{3,2,1,0:T(8,128)(2,1)} %refs_4_.1, ...), custom_call_target="tpu_custom_call" | custom-call | flops 24159191040 | bytes 251658240 | tf_op jit(solution)/shard_map/ladder/pallas_call | solution.py:298
  359.4 11.3 %copy.9 = bf16[6,96,64,128]{3,2,1,0:T(8,128)(2,1)} copy(bf16[6,96,64,128]{3,2,1,0:T(8,128)(2,1)} %get-tuple-element.6) | data formatting | bytes 18874368

commit v2 on v1

--- a/solution.py
+++ b/solution.py
@@ -127,11 +127,19 @@
     lax.fori_loop(0, pairs, one, 0)
 
 
+def meet(level, low, mine, partner, dtype):
+    return ((mine + partner) / (level - low)).astype(dtype)
+
+
+def spread(virt_row, table):
+    table[...] = jnp.broadcast_to(virt_row[...], table.shape).T
+
+
 def fused_kernel(pairs, virts, *refs):
-    tiles, occ_own, occ_all, amplitudes, weights, virt_own, virt_all = refs[:7]
-    out, codes_far, scales_far = refs[7:10]
-    own, other, picked, ladder, codes, scales, arrived, sizes, results = refs[10:19]
-    own_sem, swap_send, swap_recv, hop, send, recv, send_s, recv_s, out_sem = refs[19:]
+    tiles, counts, occupied, amplitudes, weights, virt_row = refs[:6]
+    part, last, arrived, sizes, codes_far, scales_far = refs[6:12]
+    own, other, picked, ladder, codes, scales, got_codes, got_sizes, results, table = refs[12:22]
+    own_sem, swap_send, swap_recv, hop, send, recv, send_s, recv_s, out_sem, last_sem = refs[22:]
     r, k = pl.program_id(0), pl.program_id(1)
     rows, steps = pl.num_programs(0), pl.num_programs(1)
     chunks, others, held, depth = amplitudes.shape
@@ -140,6 +148,7 @@
     p, v = lax.axis_index("pair"), lax.axis_index("virt")
     me = p * virts + v
     duos = codes.shape[1]
+    early = chunks - 1
 
     def own_copy(x):
         return pltpu.make_async_copy(amplitudes.at[x], own, own_sem)
@@ -154,23 +163,35 @@
             device_id_type=MESH,
         )
 
-    def moves(x, d):
-        t = lax.rem(me + d, count)
-        target = (t // virts, lax.rem(t, virts))
-        return [
+    def send_to(x, q, w):
+        for source, land, sent, got in (
+            (codes_far, arrived, send, recv),
+            (scales_far, sizes, send_s, recv_s),
+        ):
             pltpu.make_async_remote_copy(
-                src_ref=source.at[x, t],
+                src_ref=source.at[x, q * virts + w],
                 dst_ref=land.at[x, me],
                 send_sem=sent.at[x],
                 recv_sem=got.at[x],
-                device_id=target,
+                device_id=(q, w),
                 device_id_type=MESH,
-            )
-            for source, land, sent, got in (
-                (codes_far, arrived, send, recv),
-                (scales_far, sizes, send_s, recv_s),
-            )
-        ]
+            ).start()
+
+    def send_near(x):
+        def begin(d, _):
+            send_to(x, lax.rem(p + d, pairs), v)
+            return 0
+
+        lax.fori_loop(1, pairs, begin, 0)
+        pltpu.make_async_copy(codes_far.at[x, me], arrived.at[x, me], recv.at[x]).start()
+        pltpu.make_async_copy(scales_far.at[x, me], sizes.at[x, me], recv_s.at[x]).start()
+
+    def send_across(x):
+        def begin(d, _):
+            send_to(x, lax.rem(p + d, pairs), 1 - v)
+            return 0
+
+        lax.fori_loop(0, pairs, begin, 0)
 
     @pl.when((r == 0) & (k == 0))
     def _():
@@ -179,6 +200,7 @@
         for x in range(chunks):
             swap(x).start()
         picked[2 * held] = jnp.zeros((others, depth), picked.dtype)
+        spread(virt_row, table)
 
     @pl.when(k == 0)
     def _():
@@ -191,11 +213,25 @@
         def _():
             own_copy(r + 1).start()
 
+    @pl.when((k == 0) & (r == rows - 1))
+    def _():
+        def begin(x, _):
+            send_across(x)
+            return 0
+
+        lax.fori_loop(0, early, begin, 0)
+
     for s in range(block):
         a = k * block + s
-        lhs = jnp.concatenate([picked[tiles[a, x]] for x in range(slots)], axis=1)
+        live = counts[a]
+        parts = []
+        for x in range(slots):
+            place = lax.rem(tiles[x, a] - v * held + 2 * held, 2 * held)
+            parts.append(picked[jnp.where(x < live, place, 2 * held)])
         ladder[r, pl.ds(a, others, stride=held), :] = jnp.dot(
-            lhs, weights[s].reshape(slots * depth, wide), preferred_element_type=jnp.float32
+            jnp.concatenate(parts, axis=1),
+            weights[s].reshape(slots * depth, wide),
+            preferred_element_type=jnp.float32,
         )
 
     @pl.when(k == steps - 1)
@@ -209,24 +245,29 @@
             copy.start()
         for copy in hops:
             copy.wait()
-
-        def begin(d, _):
-            for copy in moves(r, d):
-                copy.start()
-            return 0
-
-        lax.fori_loop(1, count, begin, 0)
-        pltpu.make_async_copy(codes_far.at[r, me], arrived.at[r, me], recv.at[r]).start()
-        pltpu.make_async_copy(scales_far.at[r, me], sizes.at[r, me], recv_s.at[r]).start()
+        send_near(r)
 
     @pl.when((r == rows - 1) & (k == steps - 1))
     def _():
-        low = virt_own[...] + virt_all[...]
+        send_across(early)
+        low = table[pl.ds(pl.multiple_of(v * held, 8), held), :] + virt_row[...]
+
+        def keep(q):
+            j = q * chunks + early
+            rows_of = pl.ds(pl.multiple_of(j * held, 8), held)
+            return pltpu.make_async_copy(ladder.at[:, rows_of], last.at[:, q], last_sem.at[q])
+
+        for q in range(pairs):
+            keep(q).start()
 
         def result(n):
             slot = lax.rem(n, 2)
-            j = lax.rem(n, pairs) * chunks + n // pairs
-            return pltpu.make_async_copy(results.at[slot], out.at[:, j], out_sem.at[slot])
+            j = lax.rem(n, pairs) * early + n // pairs
+            return pltpu.make_async_copy(results.at[slot], part.at[:, j], out_sem.at[slot])
+
+        def fetch(c):
+            pltpu.make_async_copy(arrived.at[c], arrived.at[c], recv.at[c]).wait()
+            pltpu.make_async_copy(sizes.at[c], sizes.at[c], recv_s.at[c]).wait()
 
         def combine(n, _):
             c, q = n // pairs, lax.rem(n, pairs)
@@ -234,8 +275,15 @@
 
             @pl.when(q == 0)
             def _():
-                pltpu.make_async_copy(arrived.at[c], arrived.at[c], recv.at[c]).wait()
-                pltpu.make_async_copy(sizes.at[c], sizes.at[c], recv_s.at[c]).wait()
+                fetch(c)
+                grab = (
+                    pltpu.make_async_copy(arrived.at[c], got_codes, hop.at[0]),
+                    pltpu.make_async_copy(sizes.at[c], got_sizes, hop.at[1]),
+                )
+                for copy in grab:
+                    copy.start()
+                for copy in grab:
+                    copy.wait()
 
             @pl.when(n >= 2)
             def _():
@@ -245,8 +293,8 @@
             for m in range(duos):
                 tile = jnp.concatenate(
                     [
-                        arrived[c, 2 * q + x, m].astype(jnp.float32)
-                        * sizes[c, 2 * q + x, pl.ds(m, 1), :]
+                        got_codes[2 * q + x, m].astype(jnp.float32)
+                        * got_sizes[2 * q + x, pl.ds(m, 1), :]
                         for x in range(virts)
                     ],
                     axis=0,
@@ -255,21 +303,52 @@
                 for e in range(2):
                     i = 2 * m + e
                     mine = ladder[i, pl.ds(pl.multiple_of(j * held, 8), held), :]
-                    level = occ_own[i] + occ_all[j]
+                    level = occupied[p * chunks + i] + occupied[j]
                     partner = turned[e * held : (e + 1) * held]
-                    results[slot, i] = ((mine + partner) / (level - low)).astype(results.dtype)
+                    results[slot, i] = meet(level, low, mine, partner, results.dtype)
             result(n).start()
             return 0
 
-        total = chunks * pairs
+        total = early * pairs
         lax.fori_loop(0, total, combine, 0)
         result(total - 2).wait()
         result(total - 1).wait()
+        for q in range(pairs):
+            keep(q).wait()
         for x in range(chunks):
             swap(x).wait_send()
             most = pl.ds(0, count - 1)
             pltpu.make_async_copy(codes_far.at[x, most], codes_far.at[x, most], send.at[x]).wait()
             pltpu.make_async_copy(scales_far.at[x, most], scales_far.at[x, most], send_s.at[x]).wait()
+        fetch(early)
+
+
+def finish_kernel(occupied, part, last, codes, sizes, virt_row, out, table):
+    q = pl.program_id(0)
+    chunks, _, held, wide = last.shape
+    early = part.shape[1]
+    virts, duos = codes.shape[1], codes.shape[2]
+    p, v = lax.axis_index("pair"), lax.axis_index("virt")
+
+    @pl.when(q == 0)
+    def _():
+        spread(virt_row, table)
+
+    low = table[pl.ds(pl.multiple_of(v * held, 8), held), :] + virt_row[...]
+    for i in range(chunks):
+        for c in range(early):
+            out[i, c] = part[i, c]
+    for m in range(duos):
+        tile = jnp.concatenate(
+            [codes[0, x, m].astype(jnp.float32) * sizes[0, x, m : m + 1, :] for x in range(virts)],
+            axis=0,
+        )
+        turned = tile.T
+        for e in range(2):
+            i = 2 * m + e
+            level = occupied[p * chunks + i] + occupied[q * chunks + early]
+            partner = turned[e * held : (e + 1) * held]
+            out[i, early] = meet(level, low, last[i, 0], partner, out.dtype)
 
 
 def per_device(amplitudes, integrals, cd_tiles, tile_counts, eps_occ, eps_virt):
@@ -283,19 +362,14 @@
     count = pairs * virts
     duos = rows // 2
     steps = held // STEP
-    first_tile = lax.axis_index("virt") * held
-    first_row = lax.axis_index("pair") * rows
-    slot_ids = lax.broadcasted_iota(jnp.int32, cd_tiles.shape, 1)
-    places = lax.rem(cd_tiles - first_tile + 2 * held, 2 * held)
-    tiles = jnp.where(slot_ids < tile_counts[:, None], places, 2 * held)
-    occ_own = lax.dynamic_slice_in_dim(eps_occ, first_row, rows)
-    virt_own = lax.dynamic_slice_in_dim(eps_virt, first_tile, held)
     anywhere = pl.BlockSpec(memory_space=pl.ANY)
     vmem = pl.BlockSpec(memory_space=pltpu.VMEM)
     code_shape = (count, duos, held, wide)
     scale_shape = (count, 8, wide)
     flops = 2 * rows * others * held * slots * depth * wide
-    out, _, _ = pl.pallas_call(
+    virt_row = eps_virt.reshape(1, wide)
+    dma = pltpu.SemaphoreType.DMA
+    part, last, arrived, sizes, _, _ = pl.pallas_call(
         functools.partial(fused_kernel, pairs, virts),
         grid_spec=pltpu.PrefetchScalarGridSpec(
             num_scalar_prefetch=3,
@@ -304,9 +378,8 @@
                 anywhere,
                 pl.BlockSpec((STEP, slots, depth, wide), lambda r, k, *_: (k, 0, 0, 0)),
                 vmem,
-                vmem,
             ],
-            out_specs=[anywhere] * 3,
+            out_specs=[anywhere] * 6,
             scratch_shapes=[
                 pltpu.VMEM((others, held, depth), amplitudes.dtype),
                 pltpu.VMEM((rows, others, held, depth), amplitudes.dtype),
@@ -314,22 +387,27 @@
                 pltpu.VMEM((rows, others * held, wide), jnp.float32),
                 pltpu.VMEM(code_shape, jnp.int16),
                 pltpu.VMEM(scale_shape, jnp.float32),
-                pltpu.VMEM((rows,) + code_shape, jnp.int16),
-                pltpu.VMEM((rows,) + scale_shape, jnp.float32),
+                pltpu.VMEM(code_shape, jnp.int16),
+                pltpu.VMEM(scale_shape, jnp.float32),
                 pltpu.VMEM((2, rows, held, wide), jnp.bfloat16),
-                pltpu.SemaphoreType.DMA,
-                pltpu.SemaphoreType.DMA((rows,)),
-                pltpu.SemaphoreType.DMA((rows,)),
-                pltpu.SemaphoreType.DMA((2,)),
-                pltpu.SemaphoreType.DMA((rows,)),
-                pltpu.SemaphoreType.DMA((rows,)),
-                pltpu.SemaphoreType.DMA((rows,)),
-                pltpu.SemaphoreType.DMA((rows,)),
-                pltpu.SemaphoreType.DMA((2,)),
+                pltpu.VMEM((wide, wide), jnp.float32),
+                dma,
+                dma((rows,)),
+                dma((rows,)),
+                dma((2,)),
+                dma((rows,)),
+                dma((rows,)),
+                dma((rows,)),
+                dma((rows,)),
+                dma((2,)),
+                dma((pairs,)),
             ],
         ),
         out_shape=[
-            jax.ShapeDtypeStruct(amplitudes.shape[:3] + (wide,), jnp.bfloat16),
+            jax.ShapeDtypeStruct((rows, others - pairs, held, wide), jnp.bfloat16),
+            jax.ShapeDtypeStruct((rows, pairs, held, wide), jnp.float32),
+            jax.ShapeDtypeStruct((rows,) + code_shape, jnp.int16),
+            jax.ShapeDtypeStruct((rows,) + scale_shape, jnp.float32),
             jax.ShapeDtypeStruct((rows,) + code_shape, jnp.int16),
             jax.ShapeDtypeStruct((rows,) + scale_shape, jnp.float32),
         ],
@@ -337,19 +415,27 @@
             flops=flops, bytes_accessed=2 * rows * integrals.size, transcendentals=0
         ),
         compiler_params=pltpu.CompilerParams(
-            vmem_limit_bytes=63 * 2**20, collective_id=0, has_side_effects=True
+            vmem_limit_bytes=60 * 2**20, collective_id=0, has_side_effects=True
         ),
         name="ladder",
-    )(
-        tiles,
-        occ_own,
-        eps_occ,
-        amplitudes,
-        integrals,
-        jnp.broadcast_to(virt_own[:, None], (held, wide)),
-        jnp.broadcast_to(eps_virt[None, :], (held, wide)),
-    )
-    return out
+    )(cd_tiles.T, tile_counts, eps_occ, amplitudes, integrals, virt_row)
+    final = rows - 1
+    return pl.pallas_call(
+        finish_kernel,
+        grid=(pairs,),
+        in_specs=[
+            pl.BlockSpec(memory_space=pltpu.SMEM),
+            pl.BlockSpec((rows, final, held, wide), lambda q: (0, q, 0, 0)),
+            pl.BlockSpec((rows, 1, held, wide), lambda q: (0, q, 0, 0)),
+            pl.BlockSpec((1, virts, duos, held, wide), lambda q: (final, q, 0, 0, 0)),
+            pl.BlockSpec((1, virts, 8, wide), lambda q: (final, q, 0, 0)),
+            vmem,
+        ],
+        out_specs=pl.BlockSpec((rows, rows, held, wide), lambda q: (0, q, 0, 0)),
+        out_shape=jax.ShapeDtypeStruct(amplitudes.shape[:3] + (wide,), jnp.bfloat16),
+        scratch_shapes=[pltpu.VMEM((wide, wide), jnp.float32)],
+        name="finish",
+    )(eps_occ, part, last, arrived, sizes, virt_row)
 
 
 def solution(mesh):

time: 375 us -> 372 us (level)
  Pallas kernels: 353 us -> 370 us
  local copies, waits for them, and re-layouts: 16 us -> 0 us
    pallas_call x0 -> x1, Pallas kernels: none -> 14 us  [per_device(): pl.pallas_call(finish_kernel, grid=(pairs,), in_specs=[pl.BlockSpec(memor...]
    unnamed x2 -> x0, local copies, waits for them, and re-layouts: 12.1 us -> none
where the time goes in v2:
time: 372 us; the launch traced here: 370 us
  Pallas kernels  370 us (99%)
    pallas_call x1, Pallas kernels, per_device(): pl.pallas_call(functools.partial(fused_kernel, pairs, virts), grid_spec=p...  356 us
    pallas_call x1, Pallas kernels, per_device(): pl.pallas_call(finish_kernel, grid=(pairs,), in_specs=[pl.BlockSpec(memor...  14 us

profile of v2, /device:TPU:11, one launch (start us, length us, event | category | flops | bytes accessed | tf_op | source)
XLA Modules:
  0.0 370.1 jit_solution(11675302608512121421)
XLA Ops:
  0.0 356.1 %ladder.1 = (bf16[6,80,64,128]{3,2,1,0:T(8,128)(2,1)}, f32[6,16,64,128]{3,2,1,0:T(8,128)}, s16[6,32,3,64,128]{4,3,2,1,0:T(8,128)(2,1)}, f32[6,32,8,128]{3,2,1,0:...) custom-call(s32[20,64]{1,0:T(8,128)} %bitcast.4, s32[64]{0:T(128)} %refs_1_.1, f32[96]{0:T(128)} %occupied.1, ...), custom_call_target="tpu_custom_call" | custom-call | flops 24159191040 | bytes 251658240 | tf_op jit(solution)/shard_map/ladder/pallas_call | solution.py:372
  356.1 14.0 %finish.1 = bf16[6,96,64,128]{3,2,1,0:T(8,128)(2,1)} custom-call(f32[96]{0:T(128)} %occupied.1, bf16[6,80,64,128]{3,2,1,0:T(8,128)(2,1)} %get-tuple-element.9.part, f32[6,16,64,128]{3,2,1,0:T(8,128)} %get-tuple-element.10.last, s16[6,32,3,64,128]{4,3,2,1,0:T(8,128)(2,1)} %get-tuple-element.11.codes, f32[6,32,8,128]{3,2,1,0:T(8,128)} %get-tuple-element.12.sizes, ...), custom_call_target="tpu_custom_call" | custom-call | tf_op jit(solution)/shard_map/finish/pallas_call | solution.py:423

commit v3 on v2

v3 whole, which is shorter than its diff:
```python
import functools

import jax
import jax.numpy as jnp
from jax import lax
from jax.experimental import pallas as pl
from jax.experimental.pallas import tpu as pltpu
from jax.sharding import PartitionSpec as P

MESH = pl.DeviceIdType.MESH
STEP = 8
PASS = 2
TOP = 32700.0
LN2 = 0.6931471805599453


def extended(cells, sides, width):
    for axis, dim in sides:
        count = lax.axis_size(axis)
        ends = count - 1
        head = lax.slice_in_dim(cells, 0, width, axis=dim)
        tail = lax.slice_in_dim(cells, cells.shape[dim] - width, cells.shape[dim], axis=dim)
        cells = jnp.concatenate(
            [
                lax.ppermute(tail, axis, [(i, (i + 1) % count) for i in range(ends)]),
                cells,
                lax.ppermute(head, axis, [((i + 1) % count, i) for i in range(ends)]),
            ],
            axis=dim,
        )
    return cells


def general_device(amplitudes, integrals, cd_tiles, tile_counts, eps_occ, eps_virt):
    own_rows = amplitudes.shape[0]
    own_tiles = amplitudes.shape[2]
    slot_count = integrals.shape[1]
    first_tile = lax.axis_index("virt") * own_tiles
    first_row = lax.axis_index("pair") * own_rows
    local_tiles = cd_tiles - first_tile + own_tiles
    slot_ids = lax.broadcasted_iota(jnp.int32, cd_tiles.shape, 1)
    kept_slots = (slot_ids < tile_counts[:, None]).astype(jnp.bfloat16)
    masked_weights = integrals * kept_slots[:, :, None, None]
    padded = extended(amplitudes, (("virt", 2),), own_tiles)
    block_width = min(4, slot_count)
    ladder = None
    for block_start in range(0, slot_count, block_width):
        block_stop = min(block_start + block_width, slot_count)
        columns = local_tiles[:, block_start:block_stop]
        picked = jnp.take(padded, columns, axis=2)
        weights = masked_weights[:, block_start:block_stop]
        term = jnp.einsum("ijasd,asdb->ijab", picked, weights, preferred_element_type=jnp.float32)
        ladder = term if ladder is None else ladder + term
    arrived_ladder = lax.all_to_all(
        lax.all_to_all(ladder, "pair", split_axis=1, concat_axis=0, tiled=True),
        "virt",
        split_axis=3,
        concat_axis=2,
        tiled=True,
    )
    partner = jnp.transpose(arrived_ladder, (1, 0, 3, 2))
    occupied_own = lax.dynamic_slice_in_dim(eps_occ, first_row, own_rows)
    virtual_own = lax.dynamic_slice_in_dim(eps_virt, first_tile, own_tiles)
    denominator = (
        occupied_own[:, None, None, None]
        + eps_occ[None, :, None, None]
        - virtual_own[None, None, :, None]
        - eps_virt[None, None, None, :]
    )
    return ((ladder + partner) / denominator).astype(jnp.bfloat16)


def greet_all(pairs, virts):
    count = pairs * virts
    me = lax.axis_index("pair") * virts + lax.axis_index("virt")
    barrier = pltpu.get_barrier_semaphore()

    def greet(d, _):
        t = lax.rem(me + d, count)
        pl.semaphore_signal(
            barrier, inc=1, device_id=(t // virts, lax.rem(t, virts)), device_id_type=MESH
        )
        return 0

    lax.fori_loop(1, count, greet, 0)
    pl.semaphore_wait(barrier, count - 1)


def turn_tiles(block, picked, first, above):
    tall, held = block.shape[0], block.shape[1]

    def turn(x, _):
        rows = pl.ds(pl.multiple_of(x * 16, 16), 16)
        below = pl.ds(pl.multiple_of(above + x * 16, 16), 16)
        for c in range(0, held, 16):
            picked[pl.ds(first + c, 16), below, :] = jnp.swapaxes(block[rows, pl.ds(c, 16), :], 0, 1)
        return 0

    lax.fori_loop(0, tall // 16, turn, 0)


def power(exponent):
    return jnp.exp(exponent * LN2)


def pack(pairs, mine, codes):
    wide = codes.shape[2]
    tail = codes.shape[1] % 16
    held = wide // 2
    duos = codes.shape[1] // held
    half = wide // 2
    low = lax.broadcasted_iota(jnp.int32, (held, wide), 1) < half
    low_row = low[:1]
    spots = lax.broadcasted_iota(jnp.int32, (tail, wide), 0)

    def swing(values, v):
        return [x if v == e else pltpu.roll(x, half, 1) for e, x in enumerate(values)]

    def one(p, _):
        notes = [jnp.zeros((tail, wide), jnp.float32)] * 2
        for m in range(duos):
            tiles, sizes = [], []
            for e in range(2):
                spot = pl.ds(pl.multiple_of((p * 2 * duos + 2 * m + e) * held, 8), held)
                tile = mine[spot, :]
                top = jnp.maximum(jnp.max(jnp.abs(tile), axis=0, keepdims=True), 1e-30)
                size = jnp.ceil(jnp.log(top) * (1 / LN2))
                tiles.append(jnp.round(tile * (TOP * power(-size))))
                sizes.append(size)
            for v in range(2):
                code = jnp.where(low, *swing(tiles, v))
                codes[2 * p + v, pl.ds(m * held, held), :] = code.astype(jnp.int32).astype(jnp.int16)
                notes[v] = jnp.where(spots == m, jnp.where(low_row, *swing(sizes, v)), notes[v])
        for v in range(2):
            last = pl.ds(duos * held, tail)
            codes[2 * p + v, last, :] = notes[v].astype(jnp.int32).astype(jnp.int16)
        return 0

    lax.fori_loop(0, pairs, one, 0)


def decode(codes, m, held, steps):
    return codes[m * held : (m + 1) * held].astype(jnp.float32) * steps[m : m + 1, :]


def meet(level, low, mine, partner, dtype):
    return ((mine + partner) / (level - low)).astype(dtype)


def spread(virt_row, table):
    table[...] = jnp.broadcast_to(virt_row[...], table.shape).T


def fused_kernel(pairs, virts, *refs):
    tiles, counts, occupied, amplitudes, weights, virt_row = refs[:6]
    part, last, arrived, codes_far = refs[6:10]
    own, other, picked, ladder, codes, got_codes, results, table = refs[10:18]
    own_sem, swap_send, swap_recv, hop, send, recv, out_sem, last_sem = refs[18:]
    g, k = pl.program_id(0), pl.program_id(1)
    passes, steps = pl.num_programs(0), pl.num_programs(1)
    chunks, others, held, depth = amplitudes.shape
    block, slots, _, wide = weights.shape
    count = pairs * virts
    p, v = lax.axis_index("pair"), lax.axis_index("virt")
    me = p * virts + v
    duos = chunks // 2
    early = chunks - 1
    strides = 4

    def own_copy(x):
        return pltpu.make_async_copy(amplitudes.at[pl.ds(x * PASS, PASS)], own, own_sem)

    def swap(x):
        return pltpu.make_async_remote_copy(
            src_ref=amplitudes.at[x],
            dst_ref=other.at[x],
            send_sem=swap_send.at[x],
            recv_sem=swap_recv.at[x],
            device_id=(p, 1 - v),
            device_id_type=MESH,
        )

    def send_to(x, q, w):
        pltpu.make_async_remote_copy(
            src_ref=codes_far.at[x, q * virts + w],
            dst_ref=arrived.at[x, me],
            send_sem=send.at[x],
            recv_sem=recv.at[x],
            device_id=(q, w),
            device_id_type=MESH,
        ).start()

    def ahead(n):
        return lax.rem(n + p, strides) * (pairs // strides) + n // strides

    def send_near(x):
        def begin(n, _):
            d = ahead(n)

            @pl.when(d > 0)
            def _():
                send_to(x, lax.rem(p + d, pairs), v)

            return 0

        lax.fori_loop(0, pairs, begin, 0)
        pltpu.make_async_copy(codes_far.at[x, me], arrived.at[x, me], recv.at[x]).start()

    def send_across(x):
        def begin(d, _):
            send_to(x, lax.rem(p + ahead(d), pairs), 1 - v)
            return 0

        lax.fori_loop(0, pairs, begin, 0)

    @pl.when((g == 0) & (k == 0))
    def _():
        own_copy(0).start()
        greet_all(pairs, virts)
        for x in range(chunks):
            swap(x).start()
        picked[2 * held] = jnp.zeros((PASS * others, depth), picked.dtype)
        spread(virt_row, table)

    @pl.when(k == 0)
    def _():
        own_copy(g).wait()
        for u in range(PASS):
            turn_tiles(own.at[u], picked, 0, u * others)
        for u in range(PASS):
            swap(g * PASS + u).wait_recv()
            turn_tiles(other.at[g * PASS + u], picked, held, u * others)

        @pl.when(g + 1 < passes)
        def _():
            own_copy(g + 1).start()

    @pl.when((k == 0) & (g == passes - 1))
    def _():
        def begin(x, _):
            send_across(x)
            return 0

        lax.fori_loop(0, chunks - PASS, begin, 0)

    for s in range(block):
        a = k * block + s
        live = counts[a]
        parts = []
        for x in range(slots):
            place = lax.rem(tiles[x, a] - v * held + 2 * held, 2 * held)
            parts.append(picked[jnp.where(x < live, place, 2 * held)])
        ladder[g, pl.ds(a, PASS * others, stride=held), :] = jnp.dot(
            jnp.concatenate(parts, axis=1),
            weights[s].reshape(slots * depth, wide),
            preferred_element_type=jnp.float32,
        )

    @pl.when(k == steps - 1)
    def _():
        def away(u, _):
            x = g * PASS + u
            rows = pl.ds(pl.multiple_of(u * others * held, 8), others * held)
            pack(pairs, ladder.at[g, rows], codes)
            copy = pltpu.make_async_copy(codes, codes_far.at[x], hop)
            copy.start()
            copy.wait()
            send_near(x)

            @pl.when(g == passes - 1)
            def _():
                send_across(x)

            return 0

        lax.fori_loop(0, PASS, away, 0)

    @pl.when((g == passes - 1) & (k == steps - 1))
    def _():
        low = table[pl.ds(pl.multiple_of(v * held, 8), held), :] + virt_row[...]

        def spot(u, j):
            return pl.ds(pl.multiple_of((u * others + j) * held, 8), held)

        def keep(u, q):
            here = ladder.at[:, spot(u, q * chunks + early)]
            return pltpu.make_async_copy(here, last.at[:, u, q], last_sem.at[u, q])

        for q in range(pairs):
            for u in range(PASS):
                keep(u, q).start()

        def result(n):
            slot = lax.rem(n, 2)
            j = lax.rem(n, pairs) * early + n // pairs
            return pltpu.make_async_copy(results.at[slot], part.at[:, j], out_sem.at[slot])

        def fetch(c):
            pltpu.make_async_copy(arrived.at[c], arrived.at[c], recv.at[c]).wait()

        def combine(n, _):
            c, q = n // pairs, lax.rem(n, pairs)
            slot = lax.rem(n, 2)

            @pl.when(q == 0)
            def _():
                fetch(c)
                copy = pltpu.make_async_copy(arrived.at[c], got_codes, hop)
                copy.start()
                copy.wait()

            @pl.when(n >= 2)
            def _():
                result(n - 2).wait()

            j = q * chunks + c
            seen = [got_codes[virts * q + x] for x in range(virts)]
            worth = [power(x[duos * held :].astype(jnp.float32)) * (1 / TOP) for x in seen]
            for m in range(duos):
                tile = jnp.concatenate(
                    [decode(x, m, held, y) for x, y in zip(seen, worth)], axis=0
                )
                turned = tile.T
                for e in range(2):
                    i = 2 * m + e
                    mine = ladder[i // PASS, spot(i % PASS, j), :]
                    level = occupied[p * chunks + i] + occupied[j]
                    partner = turned[e * held : (e + 1) * held]
                    results[slot, i] = meet(level, low, mine, partner, results.dtype)
            result(n).start()
            return 0

        total = early * pairs
        lax.fori_loop(0, total, combine, 0)
        result(total - 2).wait()
        result(total - 1).wait()
        for q in range(pairs):
            for u in range(PASS):
                keep(u, q).wait()
        for x in range(chunks):
            swap(x).wait_send()
            most = pl.ds(0, count - 1)
            pltpu.make_async_copy(codes_far.at[x, most], codes_far.at[x, most], send.at[x]).wait()
        fetch(early)


def finish_kernel(occupied, part, last, codes, virt_row, out, table):
    q = pl.program_id(0)
    chunks, _, held, wide = last.shape
    early = part.shape[1]
    virts, duos = codes.shape[1], chunks // 2
    p, v = lax.axis_index("pair"), lax.axis_index("virt")

    @pl.when(q == 0)
    def _():
        spread(virt_row, table)

    low = table[pl.ds(pl.multiple_of(v * held, 8), held), :] + virt_row[...]
    for i in range(chunks):
        for c in range(early):
            out[i, c] = part[i, c]
    seen = [codes[0, x] for x in range(virts)]
    worth = [power(x[duos * held :].astype(jnp.float32)) * (1 / TOP) for x in seen]
    for m in range(duos):
        tile = jnp.concatenate([decode(x, m, held, y) for x, y in zip(seen, worth)], axis=0)
        turned = tile.T
        for e in range(2):
            i = 2 * m + e
            level = occupied[p * chunks + i] + occupied[q * chunks + early]
            partner = turned[e * held : (e + 1) * held]
            out[i, early] = meet(level, low, last[i, 0], partner, out.dtype)


def per_device(amplitudes, integrals, cd_tiles, tile_counts, eps_occ, eps_virt):
    pairs, virts = lax.axis_size("pair"), lax.axis_size("virt")
    rows, others, held, depth = amplitudes.shape
    slots, wide = integrals.shape[1], integrals.shape[3]
    fits = virts == 2 and held % 16 == 0 and rows % PASS == 0 and rows % 2 == 0 and rows <= 16 and pairs % 4 == 0 and others % 16 == 0
    fits = fits and wide == 2 * held and wide == 128 and held % STEP == 0
    if not fits:
        return general_device(amplitudes, integrals, cd_tiles, tile_counts, eps_occ, eps_virt)
    count = pairs * virts
    duos = rows // 2
    steps = held // STEP
    anywhere = pl.BlockSpec(memory_space=pl.ANY)
    vmem = pl.BlockSpec(memory_space=pltpu.VMEM)
    code_shape = (count, duos * held + 8, wide)
    flops = 2 * rows * others * held * slots * depth * wide
    virt_row = eps_virt.reshape(1, wide)
    dma = pltpu.SemaphoreType.DMA
    part, last, arrived, _ = pl.pallas_call(
        functools.partial(fused_kernel, pairs, virts),
        grid_spec=pltpu.PrefetchScalarGridSpec(
            num_scalar_prefetch=3,
            grid=(rows // PASS, steps),
            in_specs=[
                anywhere,
                pl.BlockSpec((STEP, slots, depth, wide), lambda r, k, *_: (k, 0, 0, 0)),
                vmem,
            ],
            out_specs=[anywhere] * 4,
            scratch_shapes=[
                pltpu.VMEM((PASS, others, held, depth), amplitudes.dtype),
                pltpu.VMEM((rows, others, held, depth), amplitudes.dtype),
                pltpu.VMEM((2 * held + 1, PASS * others, depth), amplitudes.dtype),
                pltpu.VMEM((rows // PASS, PASS * others * held, wide), jnp.float32),
                pltpu.VMEM(code_shape, jnp.int16),
                pltpu.VMEM(code_shape, jnp.int16),
                pltpu.VMEM((2, rows, held, wide), jnp.bfloat16),
                pltpu.VMEM((wide, wide), jnp.float32),
                dma,
                dma((rows,)),
                dma((rows,)),
                dma,
                dma((rows,)),
                dma((rows,)),
                dma((2,)),
                dma((PASS, pairs)),
            ],
        ),
        out_shape=[
            jax.ShapeDtypeStruct((rows, others - pairs, held, wide), jnp.bfloat16),
            jax.ShapeDtypeStruct((rows // PASS, PASS, pairs, held, wide), jnp.float32),
            jax.ShapeDtypeStruct((rows,) + code_shape, jnp.int16),
            jax.ShapeDtypeStruct((rows,) + code_shape, jnp.int16),
        ],
        cost_estimate=pl.CostEstimate(
            flops=flops, bytes_accessed=2 * rows // PASS * integrals.size, transcendentals=0
        ),
        compiler_params=pltpu.CompilerParams(
            vmem_limit_bytes=60 * 2**20, collective_id=0, has_side_effects=True
        ),
        name="ladder",
    )(cd_tiles.T, tile_counts, eps_occ, amplitudes, integrals, virt_row)
    final = rows - 1
    return pl.pallas_call(
        finish_kernel,
        grid=(pairs,),
        in_specs=[
            pl.BlockSpec(memory_space=pltpu.SMEM),
            pl.BlockSpec((rows, final, held, wide), lambda q: (0, q, 0, 0)),
            pl.BlockSpec((rows, 1, held, wide), lambda q: (0, q, 0, 0)),
            pl.BlockSpec((1, virts) + code_shape[1:], lambda q: (final, q, 0, 0)),
            vmem,
        ],
        out_specs=pl.BlockSpec((rows, rows, held, wide), lambda q: (0, q, 0, 0)),
        out_shape=jax.ShapeDtypeStruct(amplitudes.shape[:3] + (wide,), jnp.bfloat16),
        scratch_shapes=[pltpu.VMEM((wide, wide), jnp.float32)],
        name="finish",
    )(eps_occ, part, last.reshape(rows, pairs, held, wide), arrived, virt_row)


def solution(mesh):
    in_specs = (
        P("pair", None, "virt", None),
        P("virt", None, None, None),
        P("virt", None),
        P("virt"),
        P(),
        P(),
    )
    out_specs = P("pair", None, "virt", None)
    return jax.shard_map(
        per_device, mesh=mesh, in_specs=in_specs, out_specs=out_specs, check_vma=False
    )
```

time: 372 us -> 373 us (level)
  no operation moved by 1% of the time
where the time goes in v3:
time: 373 us; the launch traced here: 370 us
  Pallas kernels  370 us (99%)
    pallas_call x1, Pallas kernels, per_device(): pl.pallas_call(functools.partial(fused_kernel, pairs, virts), grid_spec=p...  356 us
    pallas_call x1, Pallas kernels, per_device(): pl.pallas_call(finish_kernel, grid=(pairs,), in_specs=[pl.BlockSpec(memor...  14.1 us

profile of v3, /device:TPU:11, one launch (start us, length us, event | category | flops | bytes accessed | tf_op | source)
XLA Modules:
  0.0 369.9 jit_solution(9279980636994708046)
XLA Ops:
  0.0 355.8 %ladder.1 = (bf16[6,80,64,128]{3,2,1,0:T(8,128)(2,1)}, f32[3,2,16,64,128]{4,3,2,1,0:T(8,128)}, s16[6,32,200,128]{3,2,1,0:T(8,128)(2,1)}, s16[6,32,200,128]{3,2,1,0:T(8,128)(2,1)}) custom-call(s32[20,64]{1,0:T(8,128)} %bitcast.6, s32[64]{0:T(128)} %refs_1_.1, f32[96]{0:T(128)} %occupied.1, bf16[6,96,64,128]{3,2,1,0:T(8,128)(2,1)} %refs_3_.1, ...), custom_call_target="tpu_custom_call" | custom-call | flops 24159191040 | bytes 125829120 | tf_op jit(solution)/shard_map/ladder/pallas_call | solution.py:391
  355.8 14.1 %finish.1 = bf16[6,96,64,128]{3,2,1,0:T(8,128)(2,1)} custom-call(f32[96]{0:T(128)} %occupied.1, bf16[6,80,64,128]{3,2,1,0:T(8,128)(2,1)} %get-tuple-element.8.part, f32[6,16,64,128]{3,2,1,0:T(8,128)} %bitcast.3, s16[6,32,200,128]{3,2,1,0:T(8,128)(2,1)} %get-tuple-element.10.codes, f32[1,128]{1,0:T(1,128)} %bitcast.5), custom_call_target="tpu_custom_call" | custom-call | tf_op jit(solution)/shard_map/finish/pallas_call | solution.py:436

commit v4 on v3

v4 whole, which is shorter than its diff:
```python
import functools

import jax
import jax.numpy as jnp
from jax import lax
from jax.experimental import pallas as pl
from jax.experimental.pallas import tpu as pltpu
from jax.sharding import PartitionSpec as P

MESH = pl.DeviceIdType.MESH
NOTES = 8
STEP = 8
TOP = 32700.0
LN2 = 0.6931471805599453


def extended(cells, sides, width):
    for axis, dim in sides:
        count = lax.axis_size(axis)
        ends = count - 1
        head = lax.slice_in_dim(cells, 0, width, axis=dim)
        tail = lax.slice_in_dim(cells, cells.shape[dim] - width, cells.shape[dim], axis=dim)
        cells = jnp.concatenate(
            [
                lax.ppermute(tail, axis, [(i, (i + 1) % count) for i in range(ends)]),
                cells,
                lax.ppermute(head, axis, [((i + 1) % count, i) for i in range(ends)]),
            ],
            axis=dim,
        )
    return cells


def general_device(amplitudes, integrals, cd_tiles, tile_counts, eps_occ, eps_virt):
    own_rows = amplitudes.shape[0]
    own_tiles = amplitudes.shape[2]
    slot_count = integrals.shape[1]
    first_tile = lax.axis_index("virt") * own_tiles
    first_row = lax.axis_index("pair") * own_rows
    local_tiles = cd_tiles - first_tile + own_tiles
    slot_ids = lax.broadcasted_iota(jnp.int32, cd_tiles.shape, 1)
    kept_slots = (slot_ids < tile_counts[:, None]).astype(jnp.bfloat16)
    masked_weights = integrals * kept_slots[:, :, None, None]
    padded = extended(amplitudes, (("virt", 2),), own_tiles)
    block_width = min(4, slot_count)
    ladder = None
    for block_start in range(0, slot_count, block_width):
        block_stop = min(block_start + block_width, slot_count)
        columns = local_tiles[:, block_start:block_stop]
        picked = jnp.take(padded, columns, axis=2)
        weights = masked_weights[:, block_start:block_stop]
        term = jnp.einsum("ijasd,asdb->ijab", picked, weights, preferred_element_type=jnp.float32)
        ladder = term if ladder is None else ladder + term
    arrived_ladder = lax.all_to_all(
        lax.all_to_all(ladder, "pair", split_axis=1, concat_axis=0, tiled=True),
        "virt",
        split_axis=3,
        concat_axis=2,
        tiled=True,
    )
    partner = jnp.transpose(arrived_ladder, (1, 0, 3, 2))
    occupied_own = lax.dynamic_slice_in_dim(eps_occ, first_row, own_rows)
    virtual_own = lax.dynamic_slice_in_dim(eps_virt, first_tile, own_tiles)
    denominator = (
        occupied_own[:, None, None, None]
        + eps_occ[None, :, None, None]
        - virtual_own[None, None, :, None]
        - eps_virt[None, None, None, :]
    )
    return ((ladder + partner) / denominator).astype(jnp.bfloat16)


def greet_all(pairs, virts):
    count = pairs * virts
    me = lax.axis_index("pair") * virts + lax.axis_index("virt")
    barrier = pltpu.get_barrier_semaphore()

    def greet(d, _):
        t = lax.rem(me + d, count)
        pl.semaphore_signal(
            barrier, inc=1, device_id=(t // virts, lax.rem(t, virts)), device_id_type=MESH
        )
        return 0

    lax.fori_loop(1, count, greet, 0)
    pl.semaphore_wait(barrier, count - 1)


def turn_tiles(block, picked, first, start, size):
    tall, held = block.shape[0], block.shape[2]

    def turn(x, _):
        rows = pl.ds(pl.multiple_of(x * tall, 16), tall)
        for c in range(0, held, 16):
            picked[pl.ds(first + c, 16), rows, :] = jnp.swapaxes(block[:, x, pl.ds(c, 16), :], 0, 1)
        return 0

    lax.fori_loop(start, start + size, turn, 0)


def power(exponent):
    return jnp.exp(exponent * LN2)


def pack(pairs, mine, codes, start, size):
    wide = codes.shape[2]
    half = held = wide // 2
    duos = size // 2
    low = lax.broadcasted_iota(jnp.int32, (held, wide), 1) < half
    low_row = low[:1]
    spots = lax.broadcasted_iota(jnp.int32, (NOTES, wide), 0)

    def swing(values, v):
        return [x if v == e else pltpu.roll(x, half, 1) for e, x in enumerate(values)]

    def one(p, _):
        notes = [jnp.zeros((NOTES, wide), jnp.float32)] * 2
        for m in range(duos):
            tiles, sizes = [], []
            for e in range(2):
                at = (start + 2 * m + e) * pairs + p
                tile = mine[pl.ds(pl.multiple_of(at * held, 8), held), :]
                top = jnp.maximum(jnp.max(jnp.abs(tile), axis=0, keepdims=True), 1e-30)
                grade = jnp.ceil(jnp.log(top) * (1 / LN2))
                tiles.append(jnp.round(tile * (TOP * power(-grade))))
                sizes.append(grade)
            for v in range(2):
                code = jnp.where(low, *swing(tiles, v))
                codes[2 * p + v, pl.ds(m * held, held), :] = code.astype(jnp.int32).astype(jnp.int16)
                notes[v] = jnp.where(spots == m, jnp.where(low_row, *swing(sizes, v)), notes[v])
        for v in range(2):
            last = pl.ds(duos * held, NOTES)
            codes[2 * p + v, last, :] = notes[v].astype(jnp.int32).astype(jnp.int16)
        return 0

    lax.fori_loop(0, pairs, one, 0)


def decode(codes, m, held, steps):
    return codes[m * held : (m + 1) * held].astype(jnp.float32) * steps[m : m + 1, :]


def meet(level, low, mine, partner, dtype):
    return ((mine + partner) / (level - low)).astype(dtype)


def partners(seen, duos, held):
    tops = [power(x[duos * held : duos * held + NOTES].astype(jnp.float32)) * (1 / TOP) for x in seen]
    for m in range(duos):
        tile = jnp.concatenate([decode(x, m, held, y) for x, y in zip(seen, tops)], axis=0)
        turned = tile.T
        yield 2 * m, turned[:held]
        yield 2 * m + 1, turned[held:]


def fused_kernel(pairs, virts, cut, *refs):
    tiles, counts, occupied, amplitudes, weights, virt_row = refs[:6]
    part, last, arrived, codes_far = refs[6:10]
    own, other, picked, ladder, codes, got_codes, results, table = refs[10:18]
    own_sem, swap_send, swap_recv, hop, send, recv, out_sem, last_sem = refs[18:]
    g, k = pl.program_id(0), pl.program_id(1)
    steps = pl.num_programs(1)
    rows, _, _, held, depth = amplitudes.shape
    block, slots, _, wide = weights.shape
    others = pairs * rows
    count = pairs * virts
    p, v = lax.axis_index("pair"), lax.axis_index("virt")
    me = p * virts + v
    final = rows - 1
    strides = 4
    chunks = [(x, x, 0, rows) for x in range(final)]
    chunks += [(final, final, 0, cut), (rows, final, cut, rows - cut)]

    def own_copy(i):
        return pltpu.make_async_copy(amplitudes.at[i], own, own_sem)

    def swap(x, i, start, size):
        some = pl.ds(start, size)
        return pltpu.make_async_remote_copy(
            src_ref=amplitudes.at[i, :, some],
            dst_ref=other.at[i, :, some],
            send_sem=swap_send.at[x],
            recv_sem=swap_recv.at[x],
            device_id=(p, 1 - v),
            device_id_type=MESH,
        )

    def tall(size):
        return pl.ds(0, size // 2 * held + NOTES)

    def ahead(n):
        return lax.rem(n + p, strides) * (pairs // strides) + n // strides

    def send_to(x, size, q, w):
        pltpu.make_async_remote_copy(
            src_ref=codes_far.at[x, q * virts + w, tall(size)],
            dst_ref=arrived.at[x, me, tall(size)],
            send_sem=send.at[x],
            recv_sem=recv.at[x],
            device_id=(q, w),
            device_id_type=MESH,
        ).start()

    def send_near(x, size):
        def begin(n, _):
            d = ahead(n)

            @pl.when(d > 0)
            def _():
                send_to(x, size, lax.rem(p + d, pairs), v)

            return 0

        lax.fori_loop(0, pairs, begin, 0)
        pltpu.make_async_copy(
            codes_far.at[x, me, tall(size)], arrived.at[x, me, tall(size)], recv.at[x]
        ).start()

    def send_across(x, size):
        def begin(n, _):
            send_to(x, size, lax.rem(p + ahead(n), pairs), 1 - v)
            return 0

        lax.fori_loop(0, pairs, begin, 0)

    @pl.when((g == 0) & (k == 0))
    def _():
        own_copy(0).start()
        greet_all(pairs, virts)
        for chunk in chunks:
            swap(*chunk).start()
        picked[2 * held] = jnp.zeros((others, depth), picked.dtype)
        table[...] = jnp.broadcast_to(virt_row[...], table.shape).T

    def load(x, i, start, size):
        @pl.when(k == 0)
        def _():
            if not start:
                own_copy(i).wait()
                turn_tiles(own, picked, 0, 0, rows)

                @pl.when(i < final)
                def _():
                    own_copy(i + 1).start()

            swap(x, i, start, size).wait_recv()
            turn_tiles(other.at[i], picked, held, start, size)

    def multiply(i, start, size):
        span = pl.ds(start * pairs, size * pairs)
        for s in range(block):
            a = k * block + s
            live = counts[a]
            parts = []
            for x in range(slots):
                place = lax.rem(tiles[x, a] - v * held + 2 * held, 2 * held)
                parts.append(picked[jnp.where(x < live, place, 2 * held), span])
            first = start * pairs * held + a
            ladder[i, pl.ds(first, size * pairs, stride=held), :] = jnp.dot(
                jnp.concatenate(parts, axis=1),
                weights[s].reshape(slots * depth, wide),
                preferred_element_type=jnp.float32,
            )

    def leave(x, i, start, size):
        pack(pairs, ladder.at[i], codes, start, size)
        copy = pltpu.make_async_copy(codes.at[:, tall(size)], codes_far.at[x, :, tall(size)], hop)
        copy.start()
        copy.wait()
        send_near(x, size)

    @pl.when(g < final)
    def _():
        load(g, g, 0, rows)
        multiply(g, 0, rows)

        @pl.when(k == steps - 1)
        def _():
            leave(g, g, 0, rows)

    @pl.when(g == final)
    def _():
        load(*chunks[final])

        @pl.when(k == 0)
        def _():
            def begin(x, _):
                send_across(x, rows)
                return 0

            lax.fori_loop(0, final, begin, 0)

        multiply(final, 0, cut)

        @pl.when(k == steps - 1)
        def _():
            leave(*chunks[final])
            send_across(final, cut)

    def combine_all():
        low = table[pl.ds(pl.multiple_of(v * held, 8), held), :] + virt_row[...]
        tail = pl.ds(final * pairs * held, pairs * held)
        keep = pltpu.make_async_copy(ladder.at[pl.ds(cut, rows - cut), tail], last, last_sem)
        keep.start()

        def result(n, size):
            slot, some = lax.rem(n, 2), pl.ds(0, size)
            j = lax.rem(n, pairs) * rows + n // pairs
            return pltpu.make_async_copy(results.at[slot, some], part.at[some, j], out_sem.at[slot])

        def fetch(x, size):
            land = arrived.at[x, :, tall(size)]
            pltpu.make_async_copy(land, land, recv.at[x]).wait()

        def pull(x, size):
            fetch(x, size)
            copy = pltpu.make_async_copy(
                arrived.at[x, :, tall(size)], got_codes.at[:, tall(size)], hop
            )
            copy.start()
            copy.wait()

        def combine(n, size):
            c, q = n // pairs, lax.rem(n, pairs)
            slot = lax.rem(n, 2)
            j = q * rows + c
            seen = [got_codes[virts * q + x] for x in range(virts)]
            for i, partner in partners(seen, size // 2, held):
                mine = ladder[i, pl.ds(pl.multiple_of((c * pairs + q) * held, 8), held), :]
                level = occupied[p * rows + i] + occupied[j]
                results[slot, i] = meet(level, low, mine, partner, results.dtype)
            result(n, size).start()

        def whole(n, _):
            @pl.when(lax.rem(n, pairs) == 0)
            def _():
                pull(n // pairs, rows)

            @pl.when(n >= 2)
            def _():
                result(n - 2, rows).wait()

            combine(n, rows)
            return 0

        def some(n, _):
            @pl.when(n >= 2)
            def _():
                result(full + n - 2, cut).wait()

            combine(full + n, cut)
            return 0

        full = final * pairs
        lax.fori_loop(0, full, whole, 0)
        for n in (2, 1):
            result(full - n, rows).wait()
        pull(final, cut)
        lax.fori_loop(0, pairs, some, 0)
        for n in (2, 1):
            result(full + pairs - n, cut).wait()
        keep.wait()
        for chunk in chunks:
            x, _, _, size = chunk
            swap(*chunk).wait_send()
            sent = codes_far.at[x, pl.ds(0, count - 1), tall(size)]
            pltpu.make_async_copy(sent, sent, send.at[x]).wait()
        fetch(rows, rows - cut)

    @pl.when(g == rows)
    def _():
        load(*chunks[rows])
        multiply(final, cut, rows - cut)

        @pl.when(k == steps - 1)
        def _():
            leave(*chunks[rows])
            send_across(rows, rows - cut)
            combine_all()


def finish_kernel(occupied, part, last, codes, virt_row, out, table):
    q = pl.program_id(0)
    rows, held = part.shape[0], part.shape[2]
    left, virts = last.shape[0], codes.shape[1]
    cut, final = rows - left, rows - 1
    p, v = lax.axis_index("pair"), lax.axis_index("virt")

    @pl.when(q == 0)
    def _():
        table[...] = jnp.broadcast_to(virt_row[...], table.shape).T

    low = table[pl.ds(pl.multiple_of(v * held, 8), held), :] + virt_row[...]
    for i in range(rows):
        for c in range(rows if i < cut else final):
            out[i, c] = part[i, c]
    seen = [codes[0, x] for x in range(virts)]
    for e, partner in partners(seen, left // 2, held):
        level = occupied[p * rows + cut + e] + occupied[q * rows + final]
        out[cut + e, final] = meet(level, low, last[e, 0], partner, out.dtype)


def per_device(amplitudes, integrals, cd_tiles, tile_counts, eps_occ, eps_virt):
    pairs, virts = lax.axis_size("pair"), lax.axis_size("virt")
    rows, others, held, depth = amplitudes.shape
    slots, wide = integrals.shape[1], integrals.shape[3]
    fits = virts == 2 and held % 16 == 0 and rows % 2 == 0 and 4 <= rows <= 16
    fits = fits and pairs % 16 == 0 and wide == 2 * held and wide == 128 and held % STEP == 0
    if not fits:
        return general_device(amplitudes, integrals, cd_tiles, tile_counts, eps_occ, eps_virt)
    count = pairs * virts
    steps = held // STEP
    cut = rows - 2
    left = rows - cut
    anywhere = pl.BlockSpec(memory_space=pl.ANY)
    vmem = pl.BlockSpec(memory_space=pltpu.VMEM)
    code_shape = (count, rows // 2 * held + NOTES, wide)
    flops = 2 * rows * others * held * slots * depth * wide
    virt_row = eps_virt.reshape(1, wide)
    dma = pltpu.SemaphoreType.DMA
    parted = amplitudes.reshape(rows, pairs, rows, held, depth)
    part, last, arrived, _ = pl.pallas_call(
        functools.partial(fused_kernel, pairs, virts, cut),
        grid_spec=pltpu.PrefetchScalarGridSpec(
            num_scalar_prefetch=3,
            grid=(rows + 1, steps),
            in_specs=[
                anywhere,
                pl.BlockSpec((STEP, slots, depth, wide), lambda g, k, *_: (k, 0, 0, 0)),
                vmem,
            ],
            out_specs=[anywhere] * 4,
            scratch_shapes=[
                pltpu.VMEM((pairs, rows, held, depth), amplitudes.dtype),
                pltpu.VMEM((rows, pairs, rows, held, depth), amplitudes.dtype),
                pltpu.VMEM((2 * held + 1, others, depth), amplitudes.dtype),
                pltpu.VMEM((rows, others * held, wide), jnp.float32),
                pltpu.VMEM(code_shape, jnp.int16),
                pltpu.VMEM(code_shape, jnp.int16),
                pltpu.VMEM((2, rows, held, wide), jnp.bfloat16),
                pltpu.VMEM((wide, wide), jnp.float32),
                dma,
                dma((rows + 1,)),
                dma((rows + 1,)),
                dma,
                dma((rows + 1,)),
                dma((rows + 1,)),
                dma((2,)),
                dma,
            ],
        ),
        out_shape=[
            jax.ShapeDtypeStruct((rows, others, held, wide), jnp.bfloat16),
            jax.ShapeDtypeStruct((left, pairs * held, wide), jnp.float32),
            jax.ShapeDtypeStruct((rows + 1,) + code_shape, jnp.int16),
            jax.ShapeDtypeStruct((rows + 1,) + code_shape, jnp.int16),
        ],
        cost_estimate=pl.CostEstimate(
            flops=flops, bytes_accessed=2 * (rows + 1) * integrals.size, transcendentals=0
        ),
        compiler_params=pltpu.CompilerParams(
            vmem_limit_bytes=60 * 2**20, collective_id=0, has_side_effects=True
        ),
        name="ladder",
    )(cd_tiles.T, tile_counts, eps_occ, parted, integrals, virt_row)
    few = left // 2 * held + NOTES
    return pl.pallas_call(
        finish_kernel,
        grid=(pairs,),
        in_specs=[
            pl.BlockSpec(memory_space=pltpu.SMEM),
            pl.BlockSpec((rows, rows, held, wide), lambda q: (0, q, 0, 0)),
            pl.BlockSpec((left, 1, held, wide), lambda q: (0, q, 0, 0)),
            pl.BlockSpec((1, virts, few, wide), lambda q: (rows, q, 0, 0)),
            vmem,
        ],
        out_specs=pl.BlockSpec((rows, rows, held, wide), lambda q: (0, q, 0, 0)),
        out_shape=jax.ShapeDtypeStruct(amplitudes.shape[:3] + (wide,), jnp.bfloat16),
        scratch_shapes=[pltpu.VMEM((wide, wide), jnp.float32)],
        name="finish",
    )(eps_occ, part, last.reshape(left, pairs, held, wide), arrived, virt_row)


def solution(mesh):
    in_specs = (
        P("pair", None, "virt", None),
        P("virt", None, None, None),
        P("virt", None),
        P("virt"),
        P(),
        P(),
    )
    out_specs = P("pair", None, "virt", None)
    return jax.shard_map(
        per_device, mesh=mesh, in_specs=in_specs, out_specs=out_specs, check_vma=False
    )
```

time: 373 us -> 362 us (0.971)
  Pallas kernels: 370 us -> 359 us
    pallas_call x1, Pallas kernels: 356 us -> 345 us  [per_device(): pl.pallas_call(functools.partial(fused_kernel, pairs, virts, cut), grid_s...]
where the time goes in v4:
time: 362 us; the launch traced here: 359 us
  Pallas kernels  359 us (99%)
    pallas_call x1, Pallas kernels, per_device(): pl.pallas_call(functools.partial(fused_kernel, pairs, virts, cut), grid_s...  345 us
    pallas_call x1, Pallas kernels, per_device(): pl.pallas_call(finish_kernel, grid=(pairs,), in_specs=[pl.BlockSpec(memor...  13.5 us

profile of v4, /device:TPU:11, one launch (start us, length us, event | category | flops | bytes accessed | tf_op | source)
XLA Modules:
  0.0 359.0 jit_solution(14503194732632834931)
XLA Ops:
  0.0 345.5 %ladder.1 = (bf16[6,96,64,128]{3,2,1,0:T(8,128)(2,1)}, f32[2,1024,128]{2,1,0:T(8,128)}, s16[7,32,200,128]{3,2,1,0:T(8,128)(2,1)}, s16[7,32,200,128]{3,2,1,0:T(8,128)(2,1)}) custom-call(s32[20,64]{1,0:T(8,128)} %bitcast.8, s32[64]{0:T(128)} %refs_1_.1, f32[96]{0:T(128)} %occupied.1, bf16[6,16,6,64,128]{4,3,2,1,0:T(8,128)(2,1)} %bitcast.7, ...), custom_call_target="tpu_custom_call" | custom-call | flops 24159191040 | bytes 293601280 | tf_op jit(solution)/shard_map/ladder/pallas_call | solution.py:422
  345.5 13.5 %finish.1 = bf16[6,96,64,128]{3,2,1,0:T(8,128)(2,1)} custom-call(f32[96]{0:T(128)} %occupied.1, bf16[6,96,64,128]{3,2,1,0:T(8,128)(2,1)} %get-tuple-element.8.part, f32[2,16,64,128]{3,2,1,0:T(8,128)} %bitcast.4, s16[7,32,200,128]{3,2,1,0:T(8,128)(2,1)} %get-tuple-element.10.codes, f32[1,128]{1,0:T(1,128)} %bitcast.6), custom_call_target="tpu_custom_call" | custom-call | tf_op jit(solution)/shard_map/finish/pallas_call | solution.py:467

commit v5 on v4

--- a/solution.py
+++ b/solution.py
@@ -9,6 +9,7 @@
 
 MESH = pl.DeviceIdType.MESH
 NOTES = 8
+BESIDE = 3
 STEP = 8
 TOP = 32700.0
 LN2 = 0.6931471805599453
@@ -160,6 +161,7 @@
     own_sem, swap_send, swap_recv, hop, send, recv, out_sem, last_sem = refs[18:]
     g, k = pl.program_id(0), pl.program_id(1)
     steps = pl.num_programs(1)
+    weights_steps = amplitudes.shape[3] // weights.shape[0]
     rows, _, _, held, depth = amplitudes.shape
     block, slots, _, wide = weights.shape
     others = pairs * rows
@@ -297,51 +299,51 @@
             leave(*chunks[final])
             send_across(final, cut)
 
+    def result(n, size):
+        slot, some = lax.rem(n, 2), pl.ds(0, size)
+        j = lax.rem(n, pairs) * rows + n // pairs
+        return pltpu.make_async_copy(results.at[slot, some], part.at[some, j], out_sem.at[slot])
+
+    def fetch(x, size):
+        land = arrived.at[x, :, tall(size)]
+        pltpu.make_async_copy(land, land, recv.at[x]).wait()
+
+    def pull(x, size):
+        fetch(x, size)
+        copy = pltpu.make_async_copy(arrived.at[x, :, tall(size)], got_codes.at[:, tall(size)], hop)
+        copy.start()
+        copy.wait()
+
+    def combine(n, size):
+        low = table[pl.ds(pl.multiple_of(v * held, 8), held), :] + virt_row[...]
+        c, q = n // pairs, lax.rem(n, pairs)
+        slot = lax.rem(n, 2)
+        j = q * rows + c
+        seen = [got_codes[virts * q + x] for x in range(virts)]
+        for i, partner in partners(seen, size // 2, held):
+            mine = ladder[i, pl.ds(pl.multiple_of((c * pairs + q) * held, 8), held), :]
+            level = occupied[p * rows + i] + occupied[j]
+            results[slot, i] = meet(level, low, mine, partner, results.dtype)
+        result(n, size).start()
+
+    def whole(n, _):
+        @pl.when(lax.rem(n, pairs) == 0)
+        def _():
+            pull(n // pairs, rows)
+
+        @pl.when(n >= 2)
+        def _():
+            result(n - 2, rows).wait()
+
+        combine(n, rows)
+        return 0
+
+    share = BESIDE * pairs // weights_steps
+
     def combine_all():
-        low = table[pl.ds(pl.multiple_of(v * held, 8), held), :] + virt_row[...]
         tail = pl.ds(final * pairs * held, pairs * held)
         keep = pltpu.make_async_copy(ladder.at[pl.ds(cut, rows - cut), tail], last, last_sem)
         keep.start()
-
-        def result(n, size):
-            slot, some = lax.rem(n, 2), pl.ds(0, size)
-            j = lax.rem(n, pairs) * rows + n // pairs
-            return pltpu.make_async_copy(results.at[slot, some], part.at[some, j], out_sem.at[slot])
-
-        def fetch(x, size):
-            land = arrived.at[x, :, tall(size)]
-            pltpu.make_async_copy(land, land, recv.at[x]).wait()
-
-        def pull(x, size):
-            fetch(x, size)
-            copy = pltpu.make_async_copy(
-                arrived.at[x, :, tall(size)], got_codes.at[:, tall(size)], hop
-            )
-            copy.start()
-            copy.wait()
-
-        def combine(n, size):
-            c, q = n // pairs, lax.rem(n, pairs)
-            slot = lax.rem(n, 2)
-            j = q * rows + c
-            seen = [got_codes[virts * q + x] for x in range(virts)]
-            for i, partner in partners(seen, size // 2, held):
-                mine = ladder[i, pl.ds(pl.multiple_of((c * pairs + q) * held, 8), held), :]
-                level = occupied[p * rows + i] + occupied[j]
-                results[slot, i] = meet(level, low, mine, partner, results.dtype)
-            result(n, size).start()
-
-        def whole(n, _):
-            @pl.when(lax.rem(n, pairs) == 0)
-            def _():
-                pull(n // pairs, rows)
-
-            @pl.when(n >= 2)
-            def _():
-                result(n - 2, rows).wait()
-
-            combine(n, rows)
-            return 0
 
         def some(n, _):
             @pl.when(n >= 2)
@@ -352,7 +354,7 @@
             return 0
 
         full = final * pairs
-        lax.fori_loop(0, full, whole, 0)
+        lax.fori_loop(share * weights_steps, full, whole, 0)
         for n in (2, 1):
             result(full - n, rows).wait()
         pull(final, cut)
@@ -371,6 +373,7 @@
     def _():
         load(*chunks[rows])
         multiply(final, cut, rows - cut)
+        lax.fori_loop(k * share, (k + 1) * share, whole, 0)
 
         @pl.when(k == steps - 1)
         def _():
@@ -404,7 +407,7 @@
     pairs, virts = lax.axis_size("pair"), lax.axis_size("virt")
     rows, others, held, depth = amplitudes.shape
     slots, wide = integrals.shape[1], integrals.shape[3]
-    fits = virts == 2 and held % 16 == 0 and rows % 2 == 0 and 4 <= rows <= 16
+    fits = virts == 2 and held % 16 == 0 and rows % 2 == 0 and BESIDE < rows - 2 and rows <= 16
     fits = fits and pairs % 16 == 0 and wide == 2 * held and wide == 128 and held % STEP == 0
     if not fits:
         return general_device(amplitudes, integrals, cd_tiles, tile_counts, eps_occ, eps_virt)

time: 362 us -> 362 us (level)
  no operation moved by 1% of the time
where the time goes in v5:
time: 362 us; the launch traced here: 359 us
  Pallas kernels  359 us (99%)
    pallas_call x1, Pallas kernels, per_device(): pl.pallas_call(functools.partial(fused_kernel, pairs, virts, cut), grid_s...  346 us
    pallas_call x1, Pallas kernels, per_device(): pl.pallas_call(finish_kernel, grid=(pairs,), in_specs=[pl.BlockSpec(memor...  13.5 us

profile of v5, /device:TPU:11, one launch (start us, length us, event | category | flops | bytes accessed | tf_op | source)
XLA Modules:
  0.0 359.4 jit_solution(6518181549015725302)
XLA Ops:
  0.0 345.8 %ladder.1 = (bf16[6,96,64,128]{3,2,1,0:T(8,128)(2,1)}, f32[2,1024,128]{2,1,0:T(8,128)}, s16[7,32,200,128]{3,2,1,0:T(8,128)(2,1)}, s16[7,32,200,128]{3,2,1,0:T(8,128)(2,1)}) custom-call(s32[20,64]{1,0:T(8,128)} %bitcast.8, s32[64]{0:T(128)} %refs_1_.1, f32[96]{0:T(128)} %occupied.1, bf16[6,16,6,64,128]{4,3,2,1,0:T(8,128)(2,1)} %bitcast.7, ...), custom_call_target="tpu_custom_call" | custom-call | flops 24159191040 | bytes 293601280 | tf_op jit(solution)/shard_map/ladder/pallas_call | solution.py:425
  345.8 13.5 %finish.1 = bf16[6,96,64,128]{3,2,1,0:T(8,128)(2,1)} custom-call(f32[96]{0:T(128)} %occupied.1, bf16[6,96,64,128]{3,2,1,0:T(8,128)(2,1)} %get-tuple-element.8.part, f32[2,16,64,128]{3,2,1,0:T(8,128)} %bitcast.4, s16[7,32,200,128]{3,2,1,0:T(8,128)(2,1)} %get-tuple-element.10.codes, f32[1,128]{1,0:T(1,128)} %bitcast.6), custom_call_target="tpu_custom_call" | custom-call | tf_op jit(solution)/shard_map/finish/pallas_call | solution.py:470
